TPU v7x, 128 devices: a whole 4x4x4 slice. The times are simulated.
128 devices in a mesh: gx: 8 (over x_hi, y), gy: 16 (over x_lo, z, core).
Axes of the slice: x: 4 (x_hi: 2, x_lo: 2; x = x_hi * 2 + x_lo), y: 4, z: 4, core: 2. Of those that a mesh axis runs over, the one named last changes fastest.
Arguments:
- features: bfloat16 [32, 128, 128, 128], P('gx', 'gy'), may hold values from -6 to 6
- positions: bfloat16 [32, 128, 3, 128], P('gx', 'gy'), may hold values from 0 to 1
- neighbours: int32 [32, 128, 4], P('gx', 'gy'), may hold values from 0 to 8, as said below
- atom_counts: int32 [32, 128], P('gx', 'gy'), may hold values from 64 to 128
- radial_bins: int32 [32, 128, 4, 128], P('gx', 'gy'), may hold values from 0 to 31
- destination: int32 [32, 128], P('gx', 'gy'), may hold values from 0 to 4095, as said below
- anchor: int32 [4096], P(('gx', 'gy')), may hold values from 0 to 4095, as said below
- weights: bfloat16 [32, 128, 128], replicated, may hold values from -0.09375 to 0.09375
- cotangent: bfloat16 [4096, 128, 128], P(('gx', 'gy')), may hold values from -6 to 6
Outputs:
- updated: bfloat16 [4096, 128, 128], P(('gx', 'gy'))
- feature_grad: bfloat16 [32, 128, 128, 128], P('gx', 'gy')
- weight_grad: float32 [4096, 128], P(('gx', 'gy'))
Inputs may be any that keep to these rules, and one draw needn't show every extreme that they name: `neighbours`: entry 0 of every list is 4, the leaf itself; the other 3 entries are distinct codes 3 (dx + 1) + (dy + 1) of surrounding leaves at grid offset (dx, dy), dx and dy in -1, 0, 1, never 4. `destination`: one to one onto all 4096 owner slots; slot g belongs to device g // 32, devices numbered over gx then gy. Of one device's 32 leaves at most 1 goes to any one device, so each device sends its leaves to 32 distinct devices; and each device receives exactly 32 leaves, one from each of 32 distinct devices. The inverse of destination: anchor[destination[X, Y]] is the home id of leaf (X, Y).
All inputs are finite; a program needn't handle non-finite values.
Results may differ from a plain program's by a relative error of at most 0.0069.
Values may be sent and summed in bfloat16 or wider, within the bound.
No kernel may reach another device: no remote copies, remote signals or barrier semaphores. Data moves between devices by JAX's collectives and lax.ppermute only.
A program may use at most 128 MiB of HBM per device.

v0:
```python
import math

import jax
import jax.numpy as jnp
from jax import lax
from jax.sharding import Mesh
from jax.sharding import PartitionSpec as P

GX_GY = ("gx_0", "gx_1", "gy_0", "gy_1", "gy_2")
GX = ("gx_0", "gx_1")
GY = ("gy_0", "gy_1", "gy_2")


SHARPNESS = 2.0


def with_halo(block, sides, width):
    for axis, dim in sides:
        count = lax.axis_size(axis)
        forward = [(i, i + 1) for i in range(count - 1)]
        forward.append((count - 1, 0))
        backward = [(target, source) for source, target in forward]
        low = lax.ppermute(
            lax.slice_in_dim(block, block.shape[dim] - width, None, axis=dim), axis, forward
        )
        high = lax.ppermute(lax.slice_in_dim(block, 0, width, axis=dim), axis, backward)
        block = jnp.concatenate([low, block, high], axis=dim)
    return block


def in_blocks(value, dim, length):
    lengths = value.shape
    tiles = value.reshape(*lengths[:dim], length, lengths[dim] // length, *lengths[dim + 1 :])
    return jnp.moveaxis(tiles, dim, 0)


def scatter_pairs(value, chips, core, dim):
    sizes = (lax.axis_size(chips), lax.axis_size(core))
    tiles = in_blocks(value, dim, sizes[0] * sizes[1])
    inside = tiles.shape[1:]
    tiles = tiles.reshape(*sizes, *inside).swapaxes(0, 1).reshape(-1, *inside)
    tiles = lax.psum_scatter(tiles, core, scatter_dimension=0, tiled=True)
    return lax.psum_scatter(tiles, chips, scatter_dimension=0, tiled=True)[0]


def pairwise_coupling(receiver, sender_xyz, offset_codes):
    receiving = receiver.astype(jnp.float32)
    remote = sender_xyz.astype(jnp.float32)
    shift_x = (offset_codes // 3 - 1).astype(jnp.float32)
    shift_y = (offset_codes % 3 - 1).astype(jnp.float32)
    delta_x = remote[:, :, 0, None, :] + shift_x[:, :, None, None] - receiving[:, None, 0, :, None]
    delta_y = remote[:, :, 1, None, :] + shift_y[:, :, None, None] - receiving[:, None, 1, :, None]
    delta_z = remote[:, :, 2, None, :] - receiving[:, None, 2, :, None]
    distance = delta_x * delta_x + delta_y * delta_y + delta_z * delta_z
    slot_count = receiving.shape[-1]
    row_index = lax.broadcasted_iota(jnp.int32, (slot_count, slot_count), 0)
    col_index = lax.broadcasted_iota(jnp.int32, (slot_count, slot_count), 1)
    itself = (offset_codes == 4)[:, :, None, None] & (row_index == col_index)[None, None]
    return jnp.where(itself, 0.0, jnp.exp(-SHARPNESS * distance)).astype(jnp.bfloat16)


def slot_places(peer_of, local_key, per_peer):
    same_peer = peer_of[:, None] == peer_of[None, :]
    earlier = local_key[None, :] < local_key[:, None]
    ranking = jnp.sum((same_peer & earlier).astype(jnp.int32), axis=1)
    return peer_of * per_peer + ranking


def pack_rows(rows, places, total):
    matches = places[None, :] == jnp.arange(total, dtype=jnp.int32)[:, None]
    source = jnp.sum(
        jnp.where(matches, jnp.arange(rows.shape[0], dtype=jnp.int32)[None, :], 0), axis=1
    )
    present = jnp.any(matches, axis=1)
    return jnp.where(
        present[:, None, None], jnp.take(rows, source, axis=0), jnp.zeros((), rows.dtype)
    )


def relay(buffer):
    return lax.all_to_all(buffer, GX_GY, split_axis=0, concat_axis=0, tiled=True)


def fold_rims(extended, along, inside):
    middle = lax.slice_in_dim(extended, 2, inside + 2, axis=along)
    lowest = lax.slice_in_dim(extended, 0, 1, axis=along)
    highest = lax.slice_in_dim(extended, inside + 3, inside + 4, axis=along)
    low_pad = [(0, 0)] * extended.ndim
    high_pad = [(0, 0)] * extended.ndim
    low_pad[along] = (0, inside - 1)
    high_pad[along] = (inside - 1, 0)
    return middle + jnp.pad(lowest, low_pad) + jnp.pad(highest, high_pad)


def leaf_block(weight_total, block_data, weight_rows, radial):
    senders, sender_xyz, receiver, offset_codes, bin_index, valid_rows, home_grad = block_data
    leaf_count, neighbour_count, slot_count, channel_count = senders.shape
    coupling = pairwise_coupling(receiver, sender_xyz, offset_codes)
    tile_sums = jnp.einsum("bnij,bnjc->bnic", coupling, senders, preferred_element_type=jnp.float32)
    selection_mask = (bin_index[..., None] == jnp.arange(radial, dtype=jnp.int32)).astype(
        jnp.float32
    )
    gathered = jnp.einsum(
        "bnik,bnic->bikc",
        selection_mask,
        tile_sums,
        precision=lax.Precision.HIGHEST,
        preferred_element_type=jnp.float32,
    ).astype(jnp.bfloat16)
    flat_rows = gathered.reshape(leaf_count * slot_count, radial * channel_count)
    message = jnp.dot(flat_rows, weight_rows, preferred_element_type=jnp.float32)
    valid_col = valid_rows.reshape(-1, 1)
    outgoing = (jax.nn.silu(message) * valid_col).astype(jnp.bfloat16)
    logistic = jax.nn.sigmoid(message)
    gradient_slope = logistic * (1.0 + message * (1.0 - logistic))
    message_grad = (
        home_grad.reshape(-1, channel_count).astype(jnp.float32) * valid_col * gradient_slope
    ).astype(jnp.bfloat16)
    full_grad = lax.dot_general(
        message_grad, weight_rows, (((1,), (1,)), ((), ())), preferred_element_type=jnp.float32
    ).astype(jnp.bfloat16)
    full_grad = full_grad.reshape(leaf_count, slot_count, radial, channel_count)
    tile_grad = jnp.einsum(
        "bnik,bikc->bnic",
        selection_mask.astype(jnp.bfloat16),
        full_grad,
        preferred_element_type=jnp.float32,
    ).astype(jnp.bfloat16)
    sender_grad = jnp.einsum(
        "bnij,bnic->bnjc", coupling, tile_grad, preferred_element_type=jnp.float32
    )
    weight_term = lax.dot_general(
        flat_rows, message_grad, (((0,), (0,)), ((), ())), preferred_element_type=jnp.float32
    )
    return (
        weight_total + weight_term,
        (outgoing.reshape(leaf_count, slot_count, channel_count), sender_grad),
    )


def shards(
    features,
    positions,
    neighbours,
    atom_counts,
    radial_bins,
    destination,
    anchor,
    weights,
    cotangent,
):
    grid_rows, grid_cols, slot_count, channel_count = features.shape
    neighbour_count = neighbours.shape[2]
    radial = weights.shape[0]
    leaves = grid_rows * grid_cols
    across_gx = lax.axis_size(GX)
    across_gy = lax.axis_size(GY)
    peer_count = across_gx * across_gy
    per_peer = max(1, 2 * leaves // peer_count)
    buffer_size = peer_count * per_peer
    valid = (
        jnp.arange(slot_count, dtype=jnp.int32)[None, None, :] < atom_counts[:, :, None]
    ).astype(jnp.float32)
    masked = features * valid[..., None].astype(jnp.bfloat16)
    home_places = slot_places(
        destination.reshape(leaves) // leaves, jnp.arange(leaves, dtype=jnp.int32), per_peer
    )
    owner_places = slot_places(anchor // leaves, anchor % leaves, per_peer)
    returned = relay(pack_rows(cotangent, owner_places, buffer_size))
    home_grad = jnp.take(returned, home_places, axis=0)
    ghost_features, ghost_xyz = (
        with_halo(masked, ((GX, 0), (GY, 1)), 1),
        with_halo(positions, ((GX, 0), (GY, 1)), 1),
    )
    row_index = jnp.arange(grid_rows, dtype=jnp.int32)[:, None, None] + neighbours // 3
    col_index = jnp.arange(grid_cols, dtype=jnp.int32)[None, :, None] + neighbours % 3
    sender_index = (row_index * (grid_cols + 2) + col_index).reshape(-1)
    padded_leaves = (grid_rows + 2) * (grid_cols + 2)
    senders = jnp.take(
        ghost_features.reshape(padded_leaves, slot_count, channel_count), sender_index, axis=0
    )
    sender_xyz = jnp.take(ghost_xyz.reshape(padded_leaves, 3, slot_count), sender_index, axis=0)
    block_leaves = math.gcd(leaves, max(1, 512 // slot_count))
    block_count = leaves // block_leaves

    def into_blocks(array):
        return array.reshape((block_count, block_leaves) + array.shape[1:])

    block_data = (
        into_blocks(senders.reshape(leaves, neighbour_count, slot_count, channel_count)),
        into_blocks(sender_xyz.reshape(leaves, neighbour_count, 3, slot_count)),
        into_blocks(positions.reshape(leaves, 3, slot_count)),
        into_blocks(neighbours.reshape(leaves, neighbour_count)),
        into_blocks(radial_bins.reshape(leaves, neighbour_count, slot_count)),
        into_blocks(valid.reshape(leaves, slot_count)),
        into_blocks(home_grad),
    )
    weight_rows = weights.reshape(radial * channel_count, channel_count)

    def block_step(weight_total, block_slice):
        return leaf_block(weight_total, block_slice, weight_rows, radial)

    weight_start = jnp.zeros((radial * channel_count, channel_count), jnp.float32)
    weight_total, (home_out, sender_grad) = lax.scan(block_step, weight_start, block_data)
    home_out = home_out.reshape(leaves, slot_count, channel_count)
    arrived = relay(pack_rows(home_out, home_places, buffer_size))
    updated = jnp.take(arrived, owner_places, axis=0)
    sender_grad = sender_grad.reshape(
        grid_rows, grid_cols, neighbour_count, slot_count, channel_count
    )
    padded_grad = jnp.zeros((grid_rows + 2, grid_cols + 2, slot_count, channel_count), jnp.float32)
    for offset_code in range(9):
        picked = (neighbours == offset_code).astype(jnp.float32)
        contribution = jnp.sum(picked[..., None, None] * sender_grad, axis=2)
        first_row = offset_code // 3
        first_col = offset_code % 3
        padded_grad = padded_grad.at[
            first_row : first_row + grid_rows, first_col : first_col + grid_cols
        ].add(contribution)
    extended = with_halo(padded_grad, ((GX, 0), (GY, 1)), 1)
    folded = fold_rims(fold_rims(extended, 0, grid_rows), 1, grid_cols)
    feature_grad = (folded * valid[..., None]).astype(jnp.bfloat16)
    grad_scale = 1.0 / math.sqrt(peer_count * leaves * slot_count)
    weight_grad = scatter_pairs(
        weight_total * grad_scale, ("gx_0", "gx_1", "gy_0", "gy_1"), "gy_2", 0
    )
    return (updated, feature_grad, weight_grad)


def solution(mesh):
    split = Mesh(mesh.devices.reshape(2, 4, 2, 4, 2), ("gx_0", "gx_1", "gy_0", "gy_1", "gy_2"))
    placed = (
        P(GX, GY, None, None),
        P(GX, GY, None, None),
        P(GX, GY, None),
        P(GX, GY),
        P(GX, GY, None, None),
        P(GX, GY),
        P(GX_GY),
        P(),
        P(GX_GY, None, None),
    )
    return jax.shard_map(
        shards,
        mesh=split,
        in_specs=placed,
        out_specs=(P(GX_GY, None, None), P(GX, GY, None, None), P(GX_GY, None)),
        check_vma=False,
    )
```

profile of v0, /device:TPU:0, one launch (start us, length us, event | category | flops | bytes accessed | tf_op | source)
XLA Modules:
  0.0 798.4 jit_solution(9717721511720286784)
XLA Ops:
  9.7 4.0 collective-permute-start.1
  17.3 3.1 gather_fusion.2
  20.4 4.1 select_select_fusion.1
  24.5 9.1 %all-to-all-start = ((bf16[128,128,128]{2,1,0:T(8,128)(2,1)}), bf16[128,128,128]{2,1,0:T(8,128)(2,1)}, u32[]{:S(2)}, u32[]{:S(2)}) async-start(bf16[128,128,128]{2,1,0:T(8,128)(2,1)} %select_select_fusion.1), calls=%async_computation | async-start | bytes 8388608 | tf_op jit(solution)/shard_map/all_to_all | solution.py:81
  35.9 4.6 collective-permute-start.5
  46.6 2.9 collective-permute-start.3
  50.9 2.9 copy.106
  63.0 22.0 %collective-permute-done.3 = bf16[6,1,3,128]{3,1,2,0:T(2,128)(2,1)} collective-permute-done((bf16[6,1,3,128]{3,1,2,0:T(2,128)(2,1)}, bf16[6,1,3,128]{3,1,2,0:T(2,128)(2,1)}, u32[]{:S(2)}, u32[]{:S(2)}) %collective-permute-start.3) | collective-permute-done | bytes 4640 | tf_op jit(solution)/shard_map/ppermute | solution.py:26
  85.0 2.4 collective-permute-done.2
  91.5 2.1 collective-permute-start.7
  94.4 2.4 collective-permute-done.7
  96.8 4.0 collective-permute-done.6
  100.8 2.6 pad_maximum_fusion.1
  103.4 4.7 gather_fusion.1
  108.1 4.6 broadcast_select_fusion
  112.7 3.1 gather_fusion.3
  116.9 239.1 %while.27 = (s32[]{:T(128)}, f32[4096,128]{1,0:T(8,128)S(1)}, bf16[8,4,128,128]{3,2,1,0:T(8,128)(2,1)}, f32[8,4,4,128,128]{4,3,2,1,0:T(8,128)}, s32[8,4,4,128]{2...) while((s32[]{:T(128)}, f32[4096,128]{1,0:T(8,128)S(1)}, ...), condition=%wide.region_6.9_spmd.clone, body=%wide.region_5.8_spmd.clone.sunk | while | flops 1875275520 | bytes 66973376 | solution.py:204
  119.3 2.5 fusion.105
  123.0 7.6 convolution_convert_fusion.3
  132.6 7.1 convolution_add_fusion.2
  144.7 2.1 fusion.108
  149.2 2.5 fusion.105
  152.8 7.6 convolution_convert_fusion.3
  162.4 7.1 convolution_add_fusion.2
  174.6 2.1 fusion.108
  179.1 2.5 fusion.105
  182.7 7.6 convolution_convert_fusion.3
  192.3 7.1 convolution_add_fusion.2
  204.5 2.1 fusion.108
  209.0 2.5 fusion.105
  212.6 7.6 convolution_convert_fusion.3
  222.2 7.1 convolution_add_fusion.2
  234.4 2.1 fusion.108
  238.9 2.5 fusion.105
  242.5 7.6 convolution_convert_fusion.3
  252.1 7.1 convolution_add_fusion.2
  264.3 2.1 fusion.108
  268.8 2.5 fusion.105
  272.4 7.6 convolution_convert_fusion.3
  282.0 7.1 convolution_add_fusion.2
  294.1 2.1 fusion.108
  298.7 2.5 fusion.105
  302.3 7.6 convolution_convert_fusion.3
  311.9 7.1 convolution_add_fusion.2
  324.0 2.1 fusion.108
  328.5 2.5 fusion.105
  332.1 7.6 convolution_convert_fusion.3
  341.7 7.1 convolution_add_fusion.2
  353.9 2.1 fusion.108
  356.0 4.4 gather_fusion.4
  360.4 4.0 select_select_fusion
  364.4 5.8 all-to-all-start.1
  372.2 17.4 %multiply_reduce_fusion = (f32[8,4,128,128]{3,2,1,0:T(8,128)S(1)}, f32[8,4,128,128]{3,2,1,0:T(8,128)}, f32[8,4,128,128]{3,2,1,0:T(8,128)}, f32[8,4,128,128]{3,2,...) fusion(f32[8,4,4,128,128]{4,3,2,1,0:T(8,128)} %get-tuple-elemen, ...), kind=kLoop, calls=%fused_computation.71 | loop fusion | flops 33030144 | bytes 27267584 | tf_op jit(solution)/shard_map/reduce_sum | solution.py:214
  389.6 2.3 scatter-add.30
  393.7 2.4 fusion.46
  401.9 4.7 collective-permute-start.9
  406.6 24.3 %collective-permute-done.9 = f32[1,10,128,128]{3,2,1,0:T(8,128)S(1)} collective-permute-done((f32[1,10,128,128]{3,2,1,0:T(8,128)S(1)}, f32[1,10,128,128]{3,2,1,0:T(8,128)S(1)}, u32[]{:S(2)}, u32[]{:S(2)}) %collective-permute-start.9) | collective-permute-done | bytes 655392 | tf_op jit(solution)/shard_map/ppermute | solution.py:26
  430.9 2.8 collective-permute-done.8
  434.5 2.6 collective-permute-start.11
  437.3 6.9 collective-permute-done.11
  444.2 3.7 collective-permute-done.10
  447.9 2.4 pad_maximum_fusion
  453.0 2.9 gather_fusion.5
  457.1 334.5 %reduce-scatter.5.cloned.1.call-done = f32[1,32,128]{2,1,0:T(8,128)} async-done(((f32[64,32,128]{2,1,0:T(8,128)}), f32[1,32,128]{2,1,0:T(8,128)}) %reduce-scatter.5.cloned.1.call-update) | async-done | bytes 16400 | tf_op jit(solution)/shard_map/reduce_scatter | solution.py:43
  (331 shorter events, 128.4 us)
Async XLA Ops:
  7.2 10.2 %copy-start = (bf16[32,128,128]{2,1,0:T(8,128)(2,1)S(1)}, bf16[32,128,128]{2,1,0:T(8,128)(2,1)}, u32[]{:S(2)}) copy-start(bf16[32,128,128]{2,1,0:T(8,128)(2,1)} %param.41) | copy-start | bytes 3145732
  8.0 38.0 %collective-permute-start = (bf16[1,8,3,128]{3,1,2,0:T(8,128)(2,1)S(1)}, bf16[1,8,3,128]{3,1,2,0:T(8,128)(2,1)S(1)}, u32[]{:S(2)}, u32[]{:S(2)}) collective-permute-start(bf16[1,8,3,128]{3,1,2,0:T(8,128)(2,1)S(1)} %get-tuple-element.452), channel_id=1, source_target_pairs={{0,16},{16,32},{32,48},{48,64},{64,80},{80,96},{96,112},{112,0},{1... | collective-permute-start | bytes 18440 | tf_op jit(solution)/shard_map/ppermute | solution.py:23
  9.7 36.3 %collective-permute-start.1 = (bf16[1,8,3,128]{3,1,2,0:T(8,128)(2,1)S(1)}, bf16[1,8,3,128]{3,1,2,0:T(8,128)(2,1)S(1)}, u32[]{:S(2)}, u32[]{:S(2)}) collective-permute-start(bf16[1,8,3,128]{3,1,2,0:T(8,128)(2,1)S(1)} %get-tuple-element.451), channel_id=1, source_target_pairs={{16,0},{32,16},{48,32},{64,48},{80,64},{96,80},{112,96},{0,112},{1... | collective-permute-start | bytes 18440 | tf_op jit(solution)/shard_map/ppermute | solution.py:26
  16.6 3.8 copy-start.33
  24.5 9.1 %copy-start.26 = (s32[4,8]{1,0:T(4,128)S(1)}, s32[4,8]{1,0:T(4,128)}, u32[]{:S(2)}) copy-start(s32[4,8]{1,0:T(4,128)} %param.36) | copy-start | bytes 388
  24.5 9.8 %copy-start.14 = (bf16[4,8,128,128]{3,2,1,0:T(8,128)(2,1)S(1)}, bf16[4,8,128,128]{3,2,1,0:T(8,128)(2,1)}, u32[]{:S(2)}) copy-start(bf16[4,8,128,128]{3,2,1,0:T(8,128)(2,1)} %param.33) | copy-start | bytes 3145732
  24.5 15.9 %copy-start.16 = (s32[4,8,4]{1,2,0:T(4,128)S(1)}, s32[4,8,4]{1,2,0:T(4,128)}, u32[]{:S(2)}) copy-start(s32[4,8,4]{1,2,0:T(4,128)} %param.35) | copy-start | bytes 1540
  24.5 18.2 %copy-start.35 = (s32[4]{0:T(128)S(1)}, s32[4]{0:T(128)}, u32[]{:S(2)}) copy-start(s32[4]{0:T(128)} %constant.476.clone.1) | copy-start | bytes 52
  24.5 21.4 %copy-start.15 = (bf16[4,8,3,128]{3,1,2,0:T(8,128)(2,1)S(1)}, bf16[4,8,3,128]{3,1,2,0:T(8,128)(2,1)}, u32[]{:S(2)}) copy-start(bf16[4,8,3,128]{3,1,2,0:T(8,128)(2,1)} %param.34) | copy-start | bytes 73732
  24.5 88.1 %all-to-all-start = ((bf16[128,128,128]{2,1,0:T(8,128)(2,1)}), bf16[128,128,128]{2,1,0:T(8,128)(2,1)}, u32[]{:S(2)}, u32[]{:S(2)}) async-start(bf16[128,128,128]{2,1,0:T(8,128)(2,1)} %select_select_fusion.1), calls=%async_computation | async-start | bytes 8388608 | tf_op jit(solution)/shard_map/all_to_all | solution.py:81
  35.9 54.8 %collective-permute-start.5 = (bf16[1,8,128,128]{3,2,1,0:T(8,128)(2,1)}, bf16[1,8,128,128]{3,2,1,0:T(8,128)(2,1)S(1)}, u32[]{:S(2)}, u32[]{:S(2)}) collective-permute-start(bf16[1,8,128,128]{3,2,1,0:T(8,128)(2,1)} %get-tuple-element.448), channel_id=1, source_target_pairs={{16,0},{32,16},{48,32},{64,48},{80,64},{96,80},{112,96},{0,112},{1... | collective-permute-start | bytes 786440 | tf_op jit(solution)/shard_map/ppermute | solution.py:26
  40.5 50.2 %collective-permute-start.4 = (bf16[1,8,128,128]{3,2,1,0:T(8,128)(2,1)}, bf16[1,8,128,128]{3,2,1,0:T(8,128)(2,1)}, u32[]{:S(2)}, u32[]{:S(2)}) collective-permute-start(bf16[1,8,128,128]{3,2,1,0:T(8,128)(2,1)} %get-tuple-element.447), channel_id=1, source_target_pairs={{0,16},{16,32},{32,48},{48,64},{64,80},{80,96},{96,112},{112,0},{1... | collective-permute-start | bytes 786440 | tf_op jit(solution)/shard_map/ppermute | solution.py:23
  46.6 38.4 %collective-permute-start.3 = (bf16[6,1,3,128]{3,1,2,0:T(2,128)(2,1)}, bf16[6,1,3,128]{3,1,2,0:T(2,128)(2,1)}, u32[]{:S(2)}, u32[]{:S(2)}) collective-permute-start(bf16[6,1,3,128]{3,1,2,0:T(2,128)(2,1)} %get-tuple-element.450), channel_id=1, source_target_pairs={{1,0},{2,1},{3,2},{4,3},{5,4},{6,5},{7,6},{8,7},{9,8},{10,9},{11,1... | collective-permute-start | bytes 13832 | tf_op jit(solution)/shard_map/ppermute | solution.py:26
  49.5 37.9 %collective-permute-start.2 = (bf16[6,1,3,128]{3,1,2,0:T(2,128)(2,1)}, bf16[6,1,3,128]{3,1,2,0:T(2,128)(2,1)}, u32[]{:S(2)}, u32[]{:S(2)}) collective-permute-start(bf16[6,1,3,128]{3,1,2,0:T(2,128)(2,1)} %get-tuple-element.449), channel_id=1, source_target_pairs={{0,1},{1,2},{2,3},{3,4},{4,5},{5,6},{6,7},{7,8},{8,9},{9,10},{10,1... | collective-permute-start | bytes 13832 | tf_op jit(solution)/shard_map/ppermute | solution.py:23
  91.5 5.3 collective-permute-start.7
  93.6 7.2 collective-permute-start.6
  103.4 4.7 copy-start.25
  108.1 7.6 copy-start.29
  121.9 8.7 %copy-start.5 = (bf16[4096,128]{1,0:T(8,128)(2,1)S(1)}, bf16[4096,128]{1,0:T(8,128)(2,1)}, u32[]{:S(2)}) copy-start(bf16[4096,128]{1,0:T(8,128)(2,1)} %get-tuple-element.606) | copy-start | bytes 3145732 | tf_op jit(solution)/shard_map/while
  130.5 2.0 copy-start.2
  132.6 7.8 copy-start.6
  151.8 8.7 %copy-start.5 = (bf16[4096,128]{1,0:T(8,128)(2,1)S(1)}, bf16[4096,128]{1,0:T(8,128)(2,1)}, u32[]{:S(2)}) copy-start(bf16[4096,128]{1,0:T(8,128)(2,1)} %get-tuple-element.606) | copy-start | bytes 3145732 | tf_op jit(solution)/shard_map/while
  160.4 2.0 copy-start.2
  162.4 7.8 copy-start.6
  181.7 8.7 %copy-start.5 = (bf16[4096,128]{1,0:T(8,128)(2,1)S(1)}, bf16[4096,128]{1,0:T(8,128)(2,1)}, u32[]{:S(2)}) copy-start(bf16[4096,128]{1,0:T(8,128)(2,1)} %get-tuple-element.606) | copy-start | bytes 3145732 | tf_op jit(solution)/shard_map/while
  190.3 2.0 copy-start.2
  192.3 7.8 copy-start.6
  211.6 8.7 %copy-start.5 = (bf16[4096,128]{1,0:T(8,128)(2,1)S(1)}, bf16[4096,128]{1,0:T(8,128)(2,1)}, u32[]{:S(2)}) copy-start(bf16[4096,128]{1,0:T(8,128)(2,1)} %get-tuple-element.606) | copy-start | bytes 3145732 | tf_op jit(solution)/shard_map/while
  220.2 2.0 copy-start.2
  222.2 7.8 copy-start.6
  241.4 8.7 %copy-start.5 = (bf16[4096,128]{1,0:T(8,128)(2,1)S(1)}, bf16[4096,128]{1,0:T(8,128)(2,1)}, u32[]{:S(2)}) copy-start(bf16[4096,128]{1,0:T(8,128)(2,1)} %get-tuple-element.606) | copy-start | bytes 3145732 | tf_op jit(solution)/shard_map/while
  250.1 2.0 copy-start.2
  252.1 7.8 copy-start.6
  271.3 8.7 %copy-start.5 = (bf16[4096,128]{1,0:T(8,128)(2,1)S(1)}, bf16[4096,128]{1,0:T(8,128)(2,1)}, u32[]{:S(2)}) copy-start(bf16[4096,128]{1,0:T(8,128)(2,1)} %get-tuple-element.606) | copy-start | bytes 3145732 | tf_op jit(solution)/shard_map/while
  280.0 2.0 copy-start.2
  282.0 7.8 copy-start.6
  301.2 8.7 %copy-start.5 = (bf16[4096,128]{1,0:T(8,128)(2,1)S(1)}, bf16[4096,128]{1,0:T(8,128)(2,1)}, u32[]{:S(2)}) copy-start(bf16[4096,128]{1,0:T(8,128)(2,1)} %get-tuple-element.606) | copy-start | bytes 3145732 | tf_op jit(solution)/shard_map/while
  309.9 2.0 copy-start.2
  311.9 7.8 copy-start.6
  331.1 8.7 %copy-start.5 = (bf16[4096,128]{1,0:T(8,128)(2,1)S(1)}, bf16[4096,128]{1,0:T(8,128)(2,1)}, u32[]{:S(2)}) copy-start(bf16[4096,128]{1,0:T(8,128)(2,1)} %get-tuple-element.606) | copy-start | bytes 3145732 | tf_op jit(solution)/shard_map/while
  339.7 2.0 copy-start.2
  341.7 7.8 copy-start.6
  356.0 4.4 copy-start.28
  356.0 4.4 copy-start.32
  364.4 88.6 %all-to-all-start.1 = ((bf16[128,128,128]{2,1,0:T(8,128)(2,1)}), bf16[128,128,128]{2,1,0:T(8,128)(2,1)}, u32[]{:S(2)}, u32[]{:S(2)}) async-start(bf16[128,128,128]{2,1,0:T(8,128)(2,1)} %select_select_fusion), calls=%async_computation.1 | async-start | bytes 8388608 | tf_op jit(solution)/shard_map/all_to_all | solution.py:81
  370.2 66.9 %reduce-scatter.3.cloned.1.call-start = ((), (), s32[]{:S(2)}) async-start(), calls=%async_computation.4 | async-start | bytes 3145728 | tf_op jit(solution)/shard_map/reduce_scatter | solution.py:42
  370.5 1.7 copy-start.17
  370.5 1.7 copy-start.18
  372.1 419.5 %reduce-scatter.5.cloned.1.call-start = ((), (), s32[]{:S(2)}) async-start(), calls=%async_computation.5 | async-start | bytes 1064960 | tf_op jit(solution)/shard_map/reduce_scatter | solution.py:43
  389.6 2.3 copy-start.13
  391.9 1.8 copy-start.12
  393.6 2.4 copy-start.11
  396.6 1.8 copy-start.9
  399.0 1.7 copy-start.7
  401.8 32.7 %copy-start.3 = (f32[6,10,128,128]{3,2,1,0:T(8,128)}, f32[6,10,128,128]{3,2,1,0:T(8,128)S(1)}, u32[]{:S(2)}) copy-start(f32[6,10,128,128]{3,2,1,0:T(8,128)S(1)} %fusion.51) | copy-start | bytes 11796484
  401.9 35.3 %copy-start.34 = (s32[32]{0:T(128)S(1)}, s32[32]{0:T(128)}, u32[]{:S(2)}) copy-start(s32[32]{0:T(128)} %copy-done.33) | copy-start | bytes 388
  401.9 29.0 %collective-permute-start.9 = (f32[1,10,128,128]{3,2,1,0:T(8,128)S(1)}, f32[1,10,128,128]{3,2,1,0:T(8,128)S(1)}, u32[]{:S(2)}, u32[]{:S(2)}) collective-permute-start(f32[1,10,128,128]{3,2,1,0:T(8,128)S(1)} %get-tuple-element.444), channel_id=1, source_target_pairs={{16,0},{32,16},{48,32},{64,48},{80,64},{96,80},{112,96},{0,112},{1... | collective-permute-start | bytes 1966088 | tf_op jit(solution)/shard_map/ppermute | solution.py:26
  406.6 27.1 %collective-permute-start.8 = (f32[1,10,128,128]{3,2,1,0:T(8,128)S(1)}, f32[1,10,128,128]{3,2,1,0:T(8,128)S(1)}, u32[]{:S(2)}, u32[]{:S(2)}) collective-permute-start(f32[1,10,128,128]{3,2,1,0:T(8,128)S(1)} %get-tuple-element.443), channel_id=1, source_target_pairs={{0,16},{16,32},{32,48},{48,64},{64,80},{80,96},{96,112},{112,0},{1... | collective-permute-start | bytes 1966088 | tf_op jit(solution)/shard_map/ppermute | solution.py:23
  434.5 9.7 %collective-permute-start.11 = (f32[8,1,128,128]{3,2,1,0:T(8,128)}, f32[8,1,128,128]{3,2,1,0:T(8,128)S(1)}, u32[]{:S(2)}, u32[]{:S(2)}) collective-permute-start(f32[8,1,128,128]{3,2,1,0:T(8,128)} %get-tuple-element.442), channel_id=1, source_target_pairs={{1,0},{2,1},{3,2},{4,3},{5,4},{6,5},{7,6},{8,7},{9,8},{10,9},{11,1... | collective-permute-start | bytes 1572872 | tf_op jit(solution)/shard_map/ppermute | solution.py:26
  437.2 10.7 %collective-permute-start.10 = (f32[8,1,128,128]{3,2,1,0:T(8,128)S(1)}, f32[8,1,128,128]{3,2,1,0:T(8,128)S(1)}, u32[]{:S(2)}, u32[]{:S(2)}) collective-permute-start(f32[8,1,128,128]{3,2,1,0:T(8,128)S(1)} %get-tuple-element.441), channel_id=1, source_target_pairs={{0,1},{1,2},{2,3},{3,4},{4,5},{5,6},{6,7},{7,8},{8,9},{9,10},{10,1... | collective-permute-start | bytes 1572872 | tf_op jit(solution)/shard_map/ppermute | solution.py:23
  437.2 13.1 %copy-start.4 = (f32[6,10,128,128]{3,2,1,0:T(8,128)S(1)}, f32[6,10,128,128]{3,2,1,0:T(8,128)}, u32[]{:S(2)}) copy-start(f32[6,10,128,128]{3,2,1,0:T(8,128)} %copy-done.3) | copy-start | bytes 11796484
  437.3 13.1 %copy-start.30 = (pred[4]{0:T(512)(128)(4,1)S(1)}, pred[4]{0:T(512)(128)(4,1)}, u32[]{:S(2)}) copy-start(pred[4]{0:T(512)(128)(4,1)} %constant.482.clone.1) | copy-start | bytes 16
  451.4 4.5 copy-start.27
  451.4 340.1 %copy-start.1 = (bf16[32,128,128]{2,1,0:T(8,128)(2,1)S(1)}, bf16[32,128,128]{2,1,0:T(8,128)(2,1)}, u32[]{:S(2)}) copy-start(bf16[32,128,128]{2,1,0:T(8,128)(2,1)} %param.41) | copy-start | bytes 3145732
  (9 other events, 13.7 us)
Sparse Core Ops, SparseCore 0:
  373.4 13.5 reduce-scatter.2
  437.3 354.1 reduce-scatter.4
where the time goes:
time: 801 us; the launch traced here: 798 us
  waiting for transfers between devices  403 us (50%)
  matrix products  190 us (24%)
  local copies, waits for them, and re-layouts  86.2 us (11%)
  other arithmetic  65.9 us (8%)
  starting transfers between devices  37.6 us (5%)
  between operations  14.6 us (2%)
    reduce_scatter x1, waiting for transfers between devices, scatter_pairs(): return lax.psum_scatter(tiles, chips, scatter_dimension=0, tiled=True)[0]  334 us
    dot_general x8, matrix products, leaf_block(): jnp.einsum('bnik,bnic->bikc', selection_mask, tile_sums, precision=lax.Pr...  60.6 us
    dot_general x8, matrix products, leaf_block(): lax.dot_general(flat_rows, message_grad, (((0,), (0,)), ((), ())), prefer...  57.2 us
    ppermute x6, waiting for transfers between devices, with_halo(): lax.ppermute(lax.slice_in_dim(block, 0, width, axis=dim), axis, backward)  55.7 us
    ppermute x6, starting transfers between devices, with_halo(): lax.ppermute(lax.slice_in_dim(block, 0, width, axis=dim), axis, backward)  20.9 us
    dot_general x8, matrix products, leaf_block(): jnp.einsum('bnij,bnjc->bnic', coupling, senders, preferred_element_type=j...  20.4 us
    reduce_sum x1, other arithmetic, shards(): contribution = jnp.sum(picked[..., None, None] * sender_grad, axis=2)  17.4 us
    dot_general x8, matrix products, leaf_block(): jnp.einsum('bnij,bnic->bnjc', coupling, tile_grad, preferred_element_type...  16.7 us
  transfers between devices with their start and end apart: 16, of which 9 were waited for; matrix products, arithmetic and copies ran while one was open for 11% of the time, Pallas kernels for 0%

commit v1 on v0

v1 whole, which is shorter than its diff:
```python
import functools
import math

import jax
import jax.numpy as jnp
from jax import lax
from jax.experimental import pallas as pl
from jax.experimental.pallas import tpu as pltpu
from jax.sharding import PartitionSpec as P


AXES = ("gx", "gy")
SHARPNESS = 2.0
FAR = 9984.0
POS_ROWS = 16
BLOCK = 4
VMEM_LIMIT = 60 * 1024 * 1024

f32 = jnp.float32
bf16 = jnp.bfloat16

STEPS = ((1, 0), (-1, 0), (0, 1), (0, -1), (1, 1), (1, -1), (-1, 1), (-1, -1))


def picks(step, grid, low, span):
    if step == 0:
        return list(range(low, low + span))
    return [grid[1]] if step > 0 else [grid[0]]


def border(step, rows, cols):
    return [
        (r, c)
        for r in picks(step[0], (0, rows - 1), 0, rows)
        for c in picks(step[1], (0, cols - 1), 0, cols)
    ]


def rim(step, rows, cols):
    return [
        (r, c)
        for r in picks(step[0], (0, rows + 1), 1, rows)
        for c in picks(step[1], (0, cols + 1), 1, cols)
    ]


def vmem(*_):
    return pl.BlockSpec(memory_space=pltpu.VMEM)


def hbm(*_):
    return pl.BlockSpec(memory_space=pl.ANY)


def smem(*_):
    return pl.BlockSpec(memory_space=pltpu.SMEM)


def params(**extra):
    return pltpu.CompilerParams(vmem_limit_bytes=VMEM_LIMIT, **extra)


def pack_kernel(dims, counts, slots, features, positions, cotangent, *rest):
    rows, cols, slot_count = dims
    leaves = rows * cols
    home, *sends = rest[:9]
    packed, sem = rest[9:]
    copies = [
        pltpu.make_async_copy(cotangent.at[g], packed.at[slots[g]], sem.at[g])
        for g in range(leaves)
    ]
    for copy in copies:
        copy.start()
    lane = lax.broadcasted_iota(jnp.int32, (1, slot_count), 1)
    pad = jnp.zeros((POS_ROWS - 3, slot_count), f32)
    for r in range(rows):
        place = [positions[r, axis].astype(f32) for axis in range(3)]
        for c in range(cols):
            leaf = r * cols + c
            x = jnp.where(lane < counts[leaf], place[0][c : c + 1], FAR)
            block = jnp.concatenate([x, place[1][c : c + 1], place[2][c : c + 1], pad], axis=0)
            home[leaf, slot_count:, :] = block.astype(bf16)
    home[:, :slot_count, :] = features[...]
    for step, send in zip(STEPS, sends):
        for index, (r, c) in enumerate(border(step, rows, cols)):
            send[index] = home[r * cols + c]
    for copy in copies:
        copy.wait()


def leaf_columns(place, bins):
    return jnp.concatenate([place, bins.astype(f32)], axis=0).T


def forward_kernel(dims, codes, counts, slots, home, *rest):
    rows, cols, slot_count, channels, radial, neigh = dims
    halos = rest[:8]
    bins_ref, weights = rest[8:10]
    gathered, slope, coupling_out, packed = rest[10:14]
    ghost, message, outgoing, sem_in, sem_out = rest[14:]
    block = pl.program_id(0)
    wide = cols + 2

    @pl.when(block == 0)
    def _():
        copies = []
        for r in range(rows):
            copies.append((home.at[pl.ds(r * cols, cols)], ghost.at[pl.ds((r + 1) * wide + 1, cols)]))
        for step, halo in zip(STEPS, halos):
            spots = rim((-step[0], -step[1]), rows, cols)
            if step[1] == 0:
                first = spots[0][0] * wide + spots[0][1]
                copies.append((halo, ghost.at[pl.ds(first, cols)]))
            else:
                for index, (r, c) in enumerate(spots):
                    copies.append((halo.at[index], ghost.at[r * wide + c]))
        copies = [
            pltpu.make_async_copy(source, target, sem_in.at[index])
            for index, (source, target) in enumerate(copies)
        ]
        for copy in copies:
            copy.start()
        for copy in copies:
            copy.wait()

    row_index = lax.broadcasted_iota(jnp.int32, (slot_count, slot_count), 0)
    col_index = lax.broadcasted_iota(jnp.int32, (slot_count, slot_count), 1)

    def leaf_step(index, carry):
        leaf = block * BLOCK + index
        r = leaf // cols
        c = leaf % cols
        own = (r + 1) * wide + c + 1
        place = ghost[own, pl.ds(slot_count, POS_ROWS), :].astype(f32)
        columns = leaf_columns(place[:4], bins_ref[leaf])
        receiver = [
            jnp.broadcast_to(columns[:, axis : axis + 1], (slot_count, slot_count))
            for axis in range(3)
        ]
        bins = [
            jnp.broadcast_to(columns[:, 4 + n : 5 + n], (slot_count, channels))
            for n in range(neigh)
        ]
        tiles = []
        for n in range(neigh):
            code = codes[leaf * neigh + n]
            row_off = code // 3
            col_off = code % 3
            sender = (r + row_off) * wide + c + col_off
            remote = ghost[sender, pl.ds(slot_count, POS_ROWS), :].astype(f32)
            delta_x = (remote[0:1] + (row_off - 1).astype(f32)) - receiver[0]
            delta_y = (remote[1:2] + (col_off - 1).astype(f32)) - receiver[1]
            delta_z = remote[2:3] - receiver[2]
            distance = delta_x * delta_x + delta_y * delta_y + delta_z * delta_z
            coupling = jnp.exp(-SHARPNESS * distance)
            if n == 0:
                coupling = jnp.where(row_index == col_index, 0.0, coupling)
            coupling = coupling.astype(bf16)
            coupling_out[index * neigh + n] = coupling
            tiles.append(
                jnp.dot(coupling, ghost[sender, pl.ds(0, slot_count), :], preferred_element_type=f32)
            )
        merged = []
        for n in range(neigh):
            total = tiles[n]
            for m in range(n):
                total = total + jnp.where(bins[m] == bins[n], tiles[m], 0.0)
            merged.append(total.astype(bf16))
        marks = [value.astype(bf16) for value in bins]
        base = pl.multiple_of(index * slot_count, slot_count)
        for k in range(radial):
            value = jnp.zeros((slot_count, channels), bf16)
            for n in range(neigh):
                value = jnp.where(marks[n] == jnp.bfloat16(k), merged[n], value)
            gathered[pl.ds(base, slot_count), k * channels : (k + 1) * channels] = value
        return carry

    lax.fori_loop(0, BLOCK, leaf_step, 0)
    message[...] = jnp.dot(gathered[...], weights[...], preferred_element_type=f32)

    def sends(at):
        return [
            pltpu.make_async_copy(
                outgoing.at[index], packed.at[slots[at * BLOCK + index]], sem_out.at[index]
            )
            for index in range(BLOCK)
        ]

    @pl.when(block > 0)
    def _():
        for copy in sends(block - 1):
            copy.wait()

    for index in range(BLOCK):
        value = message[index * slot_count : (index + 1) * slot_count]
        valid = (row_index < counts[block * BLOCK + index]).astype(f32)
        logistic = 1.0 / (1.0 + jnp.exp(-value))
        outgoing[index] = (value * logistic * valid).astype(bf16)
        slope[index * slot_count : (index + 1) * slot_count] = (
            valid * logistic * (1.0 + value * (1.0 - logistic))
        )
    for copy in sends(block):
        copy.start()

    @pl.when(block == pl.num_programs(0) - 1)
    def _():
        for copy in sends(block):
            copy.wait()


def weight_kernel(dims, slots, gathered, slope, returned, mg_out, grad, home_grad, total, sem):
    leaves, slot_count, channels, radial = dims
    block = pl.program_id(0)

    @pl.when(block == 0)
    def _():
        copies = [
            pltpu.make_async_copy(returned.at[slots[leaf]], home_grad.at[leaf], sem.at[leaf])
            for leaf in range(leaves)
        ]
        for copy in copies:
            copy.start()
        for copy in copies:
            copy.wait()
        total[...] = jnp.zeros_like(total)

    incoming = home_grad[pl.ds(block * BLOCK, BLOCK)].reshape(BLOCK * slot_count, channels)
    message_grad = (incoming.astype(f32) * slope[...]).astype(bf16)
    mg_out[...] = message_grad
    total[...] += lax.dot_general(
        message_grad, gathered[...], (((0,), (0,)), ((), ())), preferred_element_type=f32
    )

    @pl.when(block == pl.num_programs(0) - 1)
    def _():
        for k in range(radial):
            grad[k * channels : (k + 1) * channels, :] = (
                total[:, k * channels : (k + 1) * channels].T.astype(grad.dtype)
            )


def backward_kernel(dims, codes, mg, coupling, bins_ref, weights, *rest):
    rows, cols, slot_count, channels, radial, neigh = dims
    own = rest[0]
    sends = rest[1:9]
    padded, full = rest[9:]
    block = pl.program_id(0)
    wide = cols + 2

    @pl.when(block == 0)
    def _():
        padded[...] = jnp.zeros_like(padded)

    full[...] = lax.dot_general(
        mg[...], weights[...], (((1,), (1,)), ((), ())), preferred_element_type=f32
    ).astype(bf16)
    half = slot_count // 2

    def leaf_step(index, carry):
        leaf = block * BLOCK + index
        r = leaf // cols
        c = leaf % cols
        columns = leaf_columns(jnp.zeros((4, slot_count), f32), bins_ref[leaf])
        marks = [
            jnp.broadcast_to(columns[:, 4 + n : 5 + n], (slot_count, channels)).astype(bf16)
            for n in range(neigh)
        ]
        parts = [[] for _ in range(neigh)]
        for part in range(2):
            base = pl.multiple_of(index * slot_count + part * half, half)
            values = [jnp.zeros((half, channels), bf16)] * neigh
            for k in range(radial):
                row = full[pl.ds(base, half), k * channels : (k + 1) * channels]
                for n in range(neigh):
                    mark = marks[n][part * half : (part + 1) * half]
                    values[n] = jnp.where(mark == jnp.bfloat16(k), row, values[n])
            for n in range(neigh):
                parts[n].append(values[n])
        for n in range(neigh):
            tile_grad = jnp.concatenate(parts[n], axis=0)
            code = codes[leaf * neigh + n]
            sender = (r + code // 3) * wide + c + code % 3
            padded[sender] += lax.dot_general(
                coupling[index * neigh + n],
                tile_grad,
                (((0,), (0,)), ((), ())),
                preferred_element_type=f32,
            )
        return carry

    lax.fori_loop(0, BLOCK, leaf_step, 0)

    @pl.when(block == pl.num_programs(0) - 1)
    def _():
        for r in range(rows):
            first = (r + 1) * wide + 1
            own[r * cols : (r + 1) * cols] = padded[first : first + cols]
        for step, send in zip(STEPS, sends):
            for index, (r, c) in enumerate(rim(step, rows, cols)):
                send[index] = padded[r * wide + c].astype(send.dtype)


def fold_kernel(dims, own, *rest):
    rows, cols = dims
    received = rest[:8]
    out, total = rest[8:]
    total[...] = own[...]
    for step, piece in zip(STEPS, received):
        for index, (r, c) in enumerate(border((-step[0], -step[1]), rows, cols)):
            total[r * cols + c] += piece[index].astype(f32)
    out[...] = total[...].astype(bf16)


def collect_kernel(leaves, slots, arrived, out, sem):
    copies = [
        pltpu.make_async_copy(arrived.at[slots[g]], out.at[g], sem.at[g]) for g in range(leaves)
    ]
    for copy in copies:
        copy.start()
    for copy in copies:
        copy.wait()


def shift(value, step, shape):
    gx, gy = shape
    pairs = [
        (i * gy + j, (i + step[0]) % gx * gy + (j + step[1]) % gy)
        for i in range(gx)
        for j in range(gy)
    ]
    return lax.ppermute(value, AXES, pairs)


def relay(buffer):
    return lax.all_to_all(buffer, AXES, split_axis=0, concat_axis=0, tiled=True)


def shards(
    features,
    positions,
    neighbours,
    atom_counts,
    radial_bins,
    destination,
    anchor,
    weights,
    cotangent,
):
    rows, cols, slot_count, channels = features.shape
    neigh = neighbours.shape[2]
    radial = weights.shape[0]
    leaves = rows * cols
    shape = (lax.axis_size("gx"), lax.axis_size("gy"))
    peers = shape[0] * shape[1]
    padded = (rows + 2) * (cols + 2)
    blocks = leaves // BLOCK
    tall = slot_count + POS_ROWS
    width = radial * channels
    any_dma = pltpu.SemaphoreType.DMA

    counts = atom_counts.reshape(leaves)
    codes = neighbours.reshape(leaves * neigh)
    home_slots = destination.reshape(leaves) // leaves
    owner_slots = anchor // leaves
    bins = radial_bins.reshape(leaves, neigh, slot_count)
    weight_rows = weights.reshape(width, channels)
    sizes = [len(border(step, rows, cols)) for step in STEPS]

    home, *rest = pl.pallas_call(
        functools.partial(pack_kernel, (rows, cols, slot_count)),
        out_shape=[jax.ShapeDtypeStruct((leaves, tall, channels), bf16)]
        + [jax.ShapeDtypeStruct((size, tall, channels), bf16) for size in sizes]
        + [jax.ShapeDtypeStruct((peers, slot_count, channels), bf16)],
        in_specs=[smem(), smem(), vmem(), vmem(), vmem()],
        out_specs=[vmem()] * 9 + [hbm()],
        scratch_shapes=[any_dma((leaves,))],
        compiler_params=params(),
        name="pack",
    )(
        counts,
        owner_slots,
        features.reshape(leaves, slot_count, channels),
        positions.transpose(0, 2, 1, 3),
        cotangent,
    )
    sends, cot_packed = rest[:8], rest[8]
    halos = []
    for send, step in zip(sends, STEPS):
        halos.append(shift(send, step, shape))
    returned = relay(cot_packed)

    gathered, slope, coupling, packed = pl.pallas_call(
        functools.partial(forward_kernel, (rows, cols, slot_count, channels, radial, neigh)),
        grid=(blocks,),
        out_shape=[
            jax.ShapeDtypeStruct((leaves * slot_count, width), bf16),
            jax.ShapeDtypeStruct((leaves * slot_count, channels), f32),
            jax.ShapeDtypeStruct((leaves * neigh, slot_count, slot_count), bf16),
            jax.ShapeDtypeStruct((peers, slot_count, channels), bf16),
        ],
        in_specs=[smem(), smem(), smem(), hbm()] + [hbm()] * 8 + [vmem(), vmem()],
        out_specs=[
            pl.BlockSpec((BLOCK * slot_count, width), lambda b: (b, 0)),
            pl.BlockSpec((BLOCK * slot_count, channels), lambda b: (b, 0)),
            pl.BlockSpec((BLOCK * neigh, slot_count, slot_count), lambda b: (b, 0, 0)),
            hbm(),
        ],
        scratch_shapes=[
            pltpu.VMEM((padded, tall, channels), bf16),
            pltpu.VMEM((BLOCK * slot_count, channels), f32),
            pltpu.VMEM((BLOCK, slot_count, channels), bf16),
            any_dma((2 * (rows + cols) + rows + 8,)),
            any_dma((BLOCK,)),
        ],
        compiler_params=params(dimension_semantics=("arbitrary",)),
        name="forward",
    )(codes, counts, home_slots, home, *halos, bins, weight_rows)

    arrived = relay(packed)

    message_grad, weight_part = pl.pallas_call(
        functools.partial(weight_kernel, (leaves, slot_count, channels, radial)),
        grid=(blocks,),
        out_shape=[
            jax.ShapeDtypeStruct((leaves * slot_count, channels), bf16),
            jax.ShapeDtypeStruct((width, channels), bf16),
        ],
        in_specs=[
            smem(),
            pl.BlockSpec((BLOCK * slot_count, width), lambda b: (b, 0)),
            pl.BlockSpec((BLOCK * slot_count, channels), lambda b: (b, 0)),
            hbm(),
        ],
        out_specs=[
            pl.BlockSpec((BLOCK * slot_count, channels), lambda b: (b, 0)),
            pl.BlockSpec((width, channels), lambda b: (0, 0)),
        ],
        scratch_shapes=[
            pltpu.VMEM((leaves, slot_count, channels), bf16),
            pltpu.VMEM((channels, width), f32),
            any_dma((leaves,)),
        ],
        compiler_params=params(dimension_semantics=("arbitrary",)),
        name="weight",
    )(home_slots, gathered, slope, returned)

    weight_pieces = relay(weight_part.reshape(peers, width // peers, channels))

    own, *grad_sends = pl.pallas_call(
        functools.partial(backward_kernel, (rows, cols, slot_count, channels, radial, neigh)),
        grid=(blocks,),
        out_shape=[jax.ShapeDtypeStruct((leaves, slot_count, channels), f32)]
        + [jax.ShapeDtypeStruct((size, slot_count, channels), bf16) for size in sizes],
        in_specs=[
            smem(),
            pl.BlockSpec((BLOCK * slot_count, channels), lambda b: (b, 0)),
            pl.BlockSpec((BLOCK * neigh, slot_count, slot_count), lambda b: (b, 0, 0)),
            vmem(),
            vmem(),
        ],
        out_specs=[vmem()] * 9,
        scratch_shapes=[
            pltpu.VMEM((padded, slot_count, channels), f32),
            pltpu.VMEM((BLOCK * slot_count, width), bf16),
        ],
        compiler_params=params(dimension_semantics=("arbitrary",)),
        name="backward",
    )(codes, message_grad, coupling, bins, weight_rows)

    received = []
    for send, step in zip(grad_sends, STEPS):
        received.append(shift(send, step, shape))
    feature_grad = pl.pallas_call(
        functools.partial(fold_kernel, (rows, cols)),
        out_shape=jax.ShapeDtypeStruct((leaves, slot_count, channels), bf16),
        in_specs=[vmem()] * 9,
        out_specs=vmem(),
        scratch_shapes=[pltpu.VMEM((leaves, slot_count, channels), f32)],
        compiler_params=params(),
        name="fold",
    )(own, *received)

    updated = pl.pallas_call(
        functools.partial(collect_kernel, leaves),
        out_shape=jax.ShapeDtypeStruct((leaves, slot_count, channels), bf16),
        in_specs=[smem(), hbm()],
        out_specs=vmem(),
        scratch_shapes=[any_dma((leaves,))],
        compiler_params=params(),
        name="collect",
    )(owner_slots, arrived)

    grad_scale = 1.0 / math.sqrt(peers * leaves * slot_count)
    weight_grad = jnp.sum(weight_pieces.astype(f32), axis=0) * grad_scale
    return updated, feature_grad.reshape(rows, cols, slot_count, channels), weight_grad


def solution(mesh):
    leaf = P("gx", "gy")
    placed = (leaf, leaf, leaf, leaf, leaf, leaf, P(AXES), P(), P(AXES))
    return jax.shard_map(
        shards,
        mesh=mesh,
        in_specs=placed,
        out_specs=(P(AXES), leaf, P(AXES)),
        check_vma=False,
    )
```

time: 801 us -> 271 us (0.34)
  waiting for transfers between devices: 403 us -> 105 us
  matrix products: 190 us -> 0 us
  Pallas kernels: 0 us -> 103 us
  local copies, waits for them, and re-layouts: 86.2 us -> 3.8 us
  other arithmetic: 65.9 us -> 2.56 us
  starting transfers between devices: 37.6 us -> 52.9 us
  between operations: 14.6 us -> 0.98 us
    reduce_scatter x2 -> x0, waiting for transfers between devices: 334 us -> none  [the longest x1 334 us: scatter_pairs(): return lax.psum_scatter(tiles, chips, scatter_dimension=0, tiled=True)[0]]
    dot_general x56 -> x0, matrix products: 190 us -> none  [the longest x8 60.6 us: leaf_block(): jnp.einsum('bnik,bnic->bikc', selection_mask, tile_sums, precision=lax.Pr...]
    pallas_call x0 -> x6, Pallas kernels: none -> 103 us  [the longest x1 41.7 us: shards(): pl.pallas_call(functools.partial(forward_kernel, (rows, cols, slot_count,...]
    all_to_all x2 -> x3, waiting for transfers between devices: 0.01 us -> 34.6 us  [relay(): return lax.all_to_all(buffer, AXES, split_axis=0, concat_axis=0, tiled=True)]
    gather x7 -> x0, local copies, waits for them, and re-layouts: 20.6 us -> none  [the longest x2 7.47 us: pack_rows(): jnp.take(rows, source, axis=0)]
    reduce_sum x5 -> x1, other arithmetic: 17.9 us -> 0.2 us  [shards(): weight_grad = jnp.sum(weight_pieces.astype(f32), axis=0) * grad_scale]
    while x56 -> x0, local copies, waits for them, and re-layouts: 15 us -> none
    select_n x12 -> x2, other arithmetic: 16.5 us -> 1.75 us  [the longest x1 1.17 us: shards(): owner_slots = anchor // leaves]
  transfers between devices with their start and end apart: 16 -> 19, of which waited for: 9 -> 7; matrix products, arithmetic and copies ran while one was open for 11% -> 1% of each run, Pallas kernels for 0% -> 37%
where the time goes in v1:
time: 271 us; the launch traced here: 268 us
  waiting for transfers between devices  105 us (39%)
  Pallas kernels  103 us (38%)
  starting transfers between devices  52.9 us (20%)
  local copies, waits for them, and re-layouts  3.8 us (1%)
    ppermute x16, waiting for transfers between devices, shift(): return lax.ppermute(value, AXES, pairs)  70.1 us
    pallas_call x1, Pallas kernels, shards(): pl.pallas_call(functools.partial(forward_kernel, (rows, cols, slot_count,...  41.7 us
    all_to_all x3, waiting for transfers between devices, relay(): return lax.all_to_all(buffer, AXES, split_axis=0, concat_axis=0, tiled=True)  34.6 us
    pallas_call x1, Pallas kernels, shards(): pl.pallas_call(functools.partial(backward_kernel, (rows, cols, slot_count...  33.8 us
    ppermute x16, starting transfers between devices, shift(): return lax.ppermute(value, AXES, pairs)  28.6 us
    all_to_all x3, starting transfers between devices, relay(): return lax.all_to_all(buffer, AXES, split_axis=0, concat_axis=0, tiled=True)  24.4 us
    pallas_call x1, Pallas kernels, shards(): pl.pallas_call(functools.partial(weight_kernel, (leaves, slot_count, chan...  17.5 us
  transfers between devices with their start and end apart: 19, of which 7 were waited for; matrix products, arithmetic and copies ran while one was open for 1% of the time, Pallas kernels for 37%

profile of v1, /device:TPU:0, one launch (start us, length us, event | category | flops | bytes accessed | tf_op | source)
XLA Modules:
  0.0 268.3 jit_solution(920923203794179680)
XLA Ops:
  0.6 1.3 reshape.31.counts
  1.9 1.2 and_select_fusion.1.slots
  3.1 4.2 %pack.1 = (bf16[32,144,128]{2,1,0:T(8,128)(2,1)}, bf16[8,144,128]{2,1,0:T(8,128)(2,1)}, bf16[8,144,128]{2,1,0:T(8,128)(2,1)}, bf16[4,144,128]{2,1,0:T(8,128)(2,1...) custom-call(s32[32]{0:T(128)} %reshape.31.counts, ...), custom_call_target="tpu_custom_call" | custom-call | tf_op jit(solution)/shard_map/pack/pallas_call | solution.py:369
  7.3 0.0 copy-start.19
  7.3 0.0 copy-start.18
  7.3 0.0 copy-start.17
  7.4 0.0 copy-start.16
  7.4 11.7 %all-to-all-start.1 = ((bf16[128,128,128]{2,1,0:T(8,128)(2,1)}), bf16[128,128,128]{2,1,0:T(8,128)(2,1)}, u32[]{:S(2)}, u32[]{:S(2)}) async-start(bf16[128,128,128]{2,1,0:T(8,128)(2,1)} %get-tuple-element.40), calls=%async_computation.1 | async-start | bytes 8388608 | tf_op jit(solution)/shard_map/all_to_all | solution.py:335
  19.1 1.0 collective-permute-start
  20.1 4.8 %collective-permute-start.1 = (bf16[8,144,128]{2,1,0:T(8,128)(2,1)S(1)}, bf16[8,144,128]{2,1,0:T(8,128)(2,1)S(1)}, u32[]{:S(2)}, u32[]{:S(2)}) collective-permute-start(bf16[8,144,128]{2,1,0:T(8,128)(2,1)S(1)} %copy-done.18), channel_id=1, source_target_pairs={{0,112},{1,113},{2,114},{3,115},{4,116},{5,117},{6,118},{7,119},{8... | collective-permute-start | bytes 884744 | tf_op jit(solution)/shard_map/ppermute | solution.py:331
  24.8 0.0 collective-permute-start.4
  24.8 1.5 collective-permute-start.5
  26.3 4.4 %collective-permute-start.6 = (bf16[1,144,128]{2,1,0:T(8,128)(2,1)S(1)}, bf16[1,144,128]{2,1,0:T(8,128)(2,1)S(1)}, u32[]{:S(2)}, u32[]{:S(2)}) collective-permute-start(bf16[1,144,128]{2,1,0:T(8,128)(2,1)S(1)} %copy-done.23), channel_id=1, source_target_pairs={{0,113},{1,114},{2,115},{3,116},{4,117},{5,118},{6,119},{7,120},{8... | collective-permute-start | bytes 110600 | tf_op jit(solution)/shard_map/ppermute | solution.py:331
  30.7 0.1 reshape.32
  30.8 47.4 %collective-permute-done.4.rest_4_ = bf16[1,144,128]{2,1,0:T(8,128)(2,1)S(1)} collective-permute-done((bf16[1,144,128]{2,1,0:T(8,128)(2,1)S(1)}, bf16[1,144,128]{2,1,0:T(8,128)(2,1)S(1)}, u32[]{:S(2)}, u32[]{:S(2)}) %collective-permute-start.4) | collective-permute-done | bytes 36896 | tf_op jit(solution)/shard_map/ppermute | solution.py:331
  78.2 1.4 collective-permute-start.7
  79.6 0.0 collective-permute-done.5.rest_5_
  79.6 0.1 collective-permute-start.2
  79.7 0.0 collective-permute-done.6.rest_6_
  79.7 3.9 %collective-permute-start.3 = (bf16[4,144,128]{2,1,0:T(8,128)(2,1)S(1)}, bf16[4,144,128]{2,1,0:T(8,128)(2,1)S(1)}, u32[]{:S(2)}, u32[]{:S(2)}) collective-permute-start(bf16[4,144,128]{2,1,0:T(8,128)(2,1)S(1)} %copy-done.20), channel_id=1, source_target_pairs={{0,15},{1,0},{2,1},{3,2},{4,3},{5,4},{6,5},{7,6},{8,7},{9,8},{10,9... | collective-permute-start | bytes 442376 | tf_op jit(solution)/shard_map/ppermute | solution.py:331
  83.6 0.6 and_select_fusion.slots
  84.2 0.1 copy.13
  84.3 0.6 reshape.30.codes
  84.9 0.0 collective-permute-done.7.rest_7_
  84.9 1.4 collective-permute-done.2.rest_2_
  86.3 0.0 collective-permute-done.3.rest_3_
  86.3 0.0 collective-permute-done.rest_0_
  86.4 0.0 copy-start
  86.4 0.0 collective-permute-done.1.rest_1_
  86.4 0.0 copy-start.1
  86.4 0.6 copy-done.4
  87.0 0.1 copy-done.5
  87.1 0.1 copy-done
  87.2 0.1 copy-done.1
  87.2 41.7 %forward.1 = (bf16[4096,4096]{1,0:T(8,128)(2,1)}, f32[4096,128]{1,0:T(8,128)}, bf16[128,128,128]{2,1,0:T(8,128)(2,1)}, bf16[128,128,128]{2,1,0:T(8,128)(2,1)}) custom-call(s32[128]{0:T(128)} %reshape.30.codes, s32[32]{0:T(128)} %reshape.31.counts, s32[32]{0:T(128)} %and_select_fusion.slots, bf16[32,144,128]{2,1,0:T(8,128)(2,1)} %get-tuple-element.28.home, ...), custom_call_target="tpu_custom_call" | custom-call | tf_op jit(solution)/shard_map/forward/pallas_call | solution.py:392
  129.0 0.0 all-to-all-done.1.returned
  129.0 7.2 %all-to-all-start = ((bf16[128,128,128]{2,1,0:T(8,128)(2,1)}), bf16[128,128,128]{2,1,0:T(8,128)(2,1)}, u32[]{:S(2)}, u32[]{:S(2)}) async-start(bf16[128,128,128]{2,1,0:T(8,128)(2,1)} %get-tuple-element.37), calls=%async_computation | async-start | bytes 8388608 | tf_op jit(solution)/shard_map/all_to_all | solution.py:335
  136.2 17.5 %weight.1 = (bf16[4096,128]{1,0:T(8,128)(2,1)}, bf16[4096,128]{1,0:T(8,128)(2,1)}) custom-call(s32[32]{0:T(128)} %and_select_fusion.slots, bf16[4096,4096]{1,0:T(8,128)(2,1)} %get-tuple-element.38.gathered, f32[4096,128]{1,0:T(8,128)} %get-tuple-element.39.slope, bf16[128,128,128]{2,1,0:T(8,128)(2,1)} %all-to-all-done.1.returned), custom_call_target="tpu_custom_call" | custom-call | tf_op jit(solution)/shard_map/weight/pallas_call | solution.py:421
  153.7 34.6 %all-to-all-done.arrived = bf16[128,128,128]{2,1,0:T(8,128)(2,1)} async-done(((bf16[128,128,128]{2,1,0:T(8,128)(2,1)}), bf16[128,128,128]{2,1,0:T(8,128)(2,1)}, u32[]{:S(2)}, u32[]{:S(2)}) %all-to-all-start) | async-done | bytes 4194336 | tf_op jit(solution)/shard_map/all_to_all | solution.py:335
  188.3 5.5 %all-to-all-start.2 = ((bf16[128,32,128]{2,1,0:T(8,128)(2,1)}), bf16[128,32,128]{2,1,0:T(8,128)(2,1)S(1)}, u32[]{:S(2)}, u32[]{:S(2)}) async-start(bf16[128,32,128]{2,1,0:T(8,128)(2,1)} %bitcast.8), calls=%async_computation.2 | async-start | bytes 2097152 | tf_op jit(solution)/shard_map/all_to_all | solution.py:335
  193.8 33.8 %backward.1 = (f32[32,128,128]{2,1,0:T(8,128)}, bf16[8,128,128]{2,1,0:T(8,128)(2,1)}, bf16[8,128,128]{2,1,0:T(8,128)(2,1)}, bf16[4,128,128]{2,1,0:T(8,128)(2,1)}...) custom-call(s32[128]{0:T(128)} %reshape.30.codes, ...), custom_call_target="tpu_custom_call" | custom-call | tf_op jit(solution)/shard_map/backward/pallas_call | solution.py:449
  227.6 1.0 collective-permute-start.8
  228.7 4.7 %collective-permute-start.9 = (bf16[8,128,128]{2,1,0:T(8,128)(2,1)}, bf16[8,128,128]{2,1,0:T(8,128)(2,1)S(1)}, u32[]{:S(2)}, u32[]{:S(2)}) collective-permute-start(bf16[8,128,128]{2,1,0:T(8,128)(2,1)} %get-tuple-element.45), channel_id=1, source_target_pairs={{0,112},{1,113},{2,114},{3,115},{4,116},{5,117},{6,118},{7,119},{8... | collective-permute-start | bytes 786440 | tf_op jit(solution)/shard_map/ppermute | solution.py:331
  233.4 0.0 collective-permute-start.12
  233.4 3.9 %collective-permute-start.11 = (bf16[4,128,128]{2,1,0:T(8,128)(2,1)}, bf16[4,128,128]{2,1,0:T(8,128)(2,1)S(1)}, u32[]{:S(2)}, u32[]{:S(2)}) collective-permute-start(bf16[4,128,128]{2,1,0:T(8,128)(2,1)} %get-tuple-element.47), channel_id=1, source_target_pairs={{0,15},{1,0},{2,1},{3,2},{4,3},{5,4},{6,5},{7,6},{8,7},{9,8},{10,9... | collective-permute-start | bytes 393224 | tf_op jit(solution)/shard_map/ppermute | solution.py:331
  237.2 5.6 %collective-permute-done.12.rest_4_ = bf16[1,128,128]{2,1,0:T(8,128)(2,1)S(1)} collective-permute-done((bf16[1,128,128]{2,1,0:T(8,128)(2,1)}, bf16[1,128,128]{2,1,0:T(8,128)(2,1)S(1)}, u32[]{:S(2)}, u32[]{:S(2)}) %collective-permute-start.12) | collective-permute-done | bytes 32800 | tf_op jit(solution)/shard_map/ppermute | solution.py:331
  242.8 0.0 collective-permute-start.13
  242.8 7.2 %collective-permute-done.13.rest_5_ = bf16[1,128,128]{2,1,0:T(8,128)(2,1)S(1)} collective-permute-done((bf16[1,128,128]{2,1,0:T(8,128)(2,1)}, bf16[1,128,128]{2,1,0:T(8,128)(2,1)S(1)}, u32[]{:S(2)}, u32[]{:S(2)}) %collective-permute-start.13) | collective-permute-done | bytes 32800 | tf_op jit(solution)/shard_map/ppermute | solution.py:331
  250.0 0.0 collective-permute-start.14
  250.0 6.6 %collective-permute-done.14.rest_6_ = bf16[1,128,128]{2,1,0:T(8,128)(2,1)S(1)} collective-permute-done((bf16[1,128,128]{2,1,0:T(8,128)(2,1)}, bf16[1,128,128]{2,1,0:T(8,128)(2,1)S(1)}, u32[]{:S(2)}, u32[]{:S(2)}) %collective-permute-start.14) | collective-permute-done | bytes 32800 | tf_op jit(solution)/shard_map/ppermute | solution.py:331
  256.6 2.1 collective-permute-start.15
  258.6 1.9 collective-permute-done.15.rest_7_
  260.6 0.0 collective-permute-done.8.rest_0_
  260.6 0.0 copy-start.2
  260.6 0.5 copy-done.15
  261.1 0.1 copy-done.6
  261.2 0.0 copy-done.7
  261.3 0.1 copy-done.2
  261.3 0.1 copy-done.3
  261.4 3.0 %fold.1 = bf16[32,128,128]{2,1,0:T(8,128)(2,1)} custom-call(f32[32,128,128]{2,1,0:T(8,128)} %get-tuple-element.43.own, bf16[8,128,128]{2,1,0:T(8,128)(2,1)} %copy-done.2, bf16[8,128,128]{2,1,0:T(8,128)(2,1)} %copy-done.3, bf16[4,128,128]{2,1,0:T(8,128)(2,1)} %copy-done.6, bf16[4,128,128]{2,1,0:T(8,128)(2,1)} %copy-done.7, bf16[1,128,128]{2,1,0:T(8,128)(2,1)} %copy-done.12, ...), custom_call_target="tpu_custom_call" | custom-call | tf_op jit(solution)/shard_map/fold/pallas_call | solution.py:473
  264.4 3.1 %collect.1 = bf16[32,128,128]{2,1,0:T(8,128)(2,1)} custom-call(s32[32]{0:T(128)} %and_select_fusion.1.slots, bf16[128,128,128]{2,1,0:T(8,128)(2,1)} %all-to-all-done.arrived), custom_call_target="tpu_custom_call" | custom-call | tf_op jit(solution)/shard_map/collect/pallas_call | solution.py:483
  267.5 0.0 all-to-all-done.2
  267.5 0.2 convert_reduce_fusion
  267.7 0.6 broadcast_multiply_fusion
  (40 shorter events, 0.1 us)
Async XLA Ops:
  7.3 11.8 %copy-start.19 = (bf16[8,144,128]{2,1,0:T(8,128)(2,1)S(1)}, bf16[8,144,128]{2,1,0:T(8,128)(2,1)}, u32[]{:S(2)}) copy-start(bf16[8,144,128]{2,1,0:T(8,128)(2,1)} %get-tuple-element.29) | copy-start | bytes 884740
  7.3 12.8 %copy-start.18 = (bf16[8,144,128]{2,1,0:T(8,128)(2,1)S(1)}, bf16[8,144,128]{2,1,0:T(8,128)(2,1)}, u32[]{:S(2)}) copy-start(bf16[8,144,128]{2,1,0:T(8,128)(2,1)} %get-tuple-element.30) | copy-start | bytes 884740
  7.3 17.5 %copy-start.25 = (bf16[1,144,128]{2,1,0:T(8,128)(2,1)S(1)}, bf16[1,144,128]{2,1,0:T(8,128)(2,1)}, u32[]{:S(2)}) copy-start(bf16[1,144,128]{2,1,0:T(8,128)(2,1)} %get-tuple-element.33) | copy-start | bytes 110596
  7.3 17.5 %copy-start.24 = (bf16[1,144,128]{2,1,0:T(8,128)(2,1)S(1)}, bf16[1,144,128]{2,1,0:T(8,128)(2,1)}, u32[]{:S(2)}) copy-start(bf16[1,144,128]{2,1,0:T(8,128)(2,1)} %get-tuple-element.34) | copy-start | bytes 110596
  7.3 19.0 %copy-start.23 = (bf16[1,144,128]{2,1,0:T(8,128)(2,1)S(1)}, bf16[1,144,128]{2,1,0:T(8,128)(2,1)}, u32[]{:S(2)}) copy-start(bf16[1,144,128]{2,1,0:T(8,128)(2,1)} %get-tuple-element.35) | copy-start | bytes 110596
  7.3 23.4 %copy-start.17 = (s32[4,8]{1,0:T(4,128)S(1)}, s32[4,8]{1,0:T(4,128)}, u32[]{:S(2)}) copy-start(s32[4,8]{1,0:T(4,128)} %param.14) | copy-start | bytes 388
  7.4 70.8 %copy-start.22 = (bf16[1,144,128]{2,1,0:T(8,128)(2,1)S(1)}, bf16[1,144,128]{2,1,0:T(8,128)(2,1)}, u32[]{:S(2)}) copy-start(bf16[1,144,128]{2,1,0:T(8,128)(2,1)} %get-tuple-element.36) | copy-start | bytes 110596
  7.4 72.2 %copy-start.21 = (bf16[4,144,128]{2,1,0:T(8,128)(2,1)S(1)}, bf16[4,144,128]{2,1,0:T(8,128)(2,1)}, u32[]{:S(2)}) copy-start(bf16[4,144,128]{2,1,0:T(8,128)(2,1)} %get-tuple-element.31) | copy-start | bytes 442372
  7.4 72.3 %copy-start.20 = (bf16[4,144,128]{2,1,0:T(8,128)(2,1)S(1)}, bf16[4,144,128]{2,1,0:T(8,128)(2,1)}, u32[]{:S(2)}) copy-start(bf16[4,144,128]{2,1,0:T(8,128)(2,1)} %get-tuple-element.32) | copy-start | bytes 442372
  7.4 76.8 %copy-start.16 = (s32[4,8,4]{1,2,0:T(4,128)S(1)}, s32[4,8,4]{1,2,0:T(4,128)}, u32[]{:S(2)}) copy-start(s32[4,8,4]{1,2,0:T(4,128)} %param.11) | copy-start | bytes 1540
  7.4 121.6 %all-to-all-start.1 = ((bf16[128,128,128]{2,1,0:T(8,128)(2,1)}), bf16[128,128,128]{2,1,0:T(8,128)(2,1)}, u32[]{:S(2)}, u32[]{:S(2)}) async-start(bf16[128,128,128]{2,1,0:T(8,128)(2,1)} %get-tuple-element.40), calls=%async_computation.1 | async-start | bytes 8388608 | tf_op jit(solution)/shard_map/all_to_all | solution.py:335
  19.1 67.2 %collective-permute-start = (bf16[8,144,128]{2,1,0:T(8,128)(2,1)S(1)}, bf16[8,144,128]{2,1,0:T(8,128)(2,1)S(1)}, u32[]{:S(2)}, u32[]{:S(2)}) collective-permute-start(bf16[8,144,128]{2,1,0:T(8,128)(2,1)S(1)} %copy-done.19), channel_id=1, source_target_pairs={{0,16},{1,17},{2,18},{3,19},{4,20},{5,21},{6,22},{7,23},{8,24},{9,... | collective-permute-start | bytes 884744 | tf_op jit(solution)/shard_map/ppermute | solution.py:331
  20.1 66.3 %collective-permute-start.1 = (bf16[8,144,128]{2,1,0:T(8,128)(2,1)S(1)}, bf16[8,144,128]{2,1,0:T(8,128)(2,1)S(1)}, u32[]{:S(2)}, u32[]{:S(2)}) collective-permute-start(bf16[8,144,128]{2,1,0:T(8,128)(2,1)S(1)} %copy-done.18), channel_id=1, source_target_pairs={{0,112},{1,113},{2,114},{3,115},{4,116},{5,117},{6,118},{7,119},{8... | collective-permute-start | bytes 884744 | tf_op jit(solution)/shard_map/ppermute | solution.py:331
  24.8 53.4 %collective-permute-start.4 = (bf16[1,144,128]{2,1,0:T(8,128)(2,1)S(1)}, bf16[1,144,128]{2,1,0:T(8,128)(2,1)S(1)}, u32[]{:S(2)}, u32[]{:S(2)}) collective-permute-start(bf16[1,144,128]{2,1,0:T(8,128)(2,1)S(1)} %copy-done.25), channel_id=1, source_target_pairs={{0,17},{1,18},{2,19},{3,20},{4,21},{5,22},{6,23},{7,24},{8,25},{9,... | collective-permute-start | bytes 110600 | tf_op jit(solution)/shard_map/ppermute | solution.py:331
  24.8 54.7 %collective-permute-start.5 = (bf16[1,144,128]{2,1,0:T(8,128)(2,1)S(1)}, bf16[1,144,128]{2,1,0:T(8,128)(2,1)S(1)}, u32[]{:S(2)}, u32[]{:S(2)}) collective-permute-start(bf16[1,144,128]{2,1,0:T(8,128)(2,1)S(1)} %copy-done.24), channel_id=1, source_target_pairs={{0,31},{1,16},{2,17},{3,18},{4,19},{5,20},{6,21},{7,22},{8,23},{9,... | collective-permute-start | bytes 110600 | tf_op jit(solution)/shard_map/ppermute | solution.py:331
  26.3 53.4 %collective-permute-start.6 = (bf16[1,144,128]{2,1,0:T(8,128)(2,1)S(1)}, bf16[1,144,128]{2,1,0:T(8,128)(2,1)S(1)}, u32[]{:S(2)}, u32[]{:S(2)}) collective-permute-start(bf16[1,144,128]{2,1,0:T(8,128)(2,1)S(1)} %copy-done.23), channel_id=1, source_target_pairs={{0,113},{1,114},{2,115},{3,116},{4,117},{5,118},{6,119},{7,120},{8... | collective-permute-start | bytes 110600 | tf_op jit(solution)/shard_map/ppermute | solution.py:331
  78.2 8.2 %copy-start.8 = (bf16[1,144,128]{2,1,0:T(8,128)(2,1)}, bf16[1,144,128]{2,1,0:T(8,128)(2,1)S(1)}, u32[]{:S(2)}) copy-start(bf16[1,144,128]{2,1,0:T(8,128)(2,1)S(1)} %collective-permute-done.4.rest_4_) | copy-start | bytes 110596
  78.2 6.7 %collective-permute-start.7 = (bf16[1,144,128]{2,1,0:T(8,128)(2,1)S(1)}, bf16[1,144,128]{2,1,0:T(8,128)(2,1)S(1)}, u32[]{:S(2)}, u32[]{:S(2)}) collective-permute-start(bf16[1,144,128]{2,1,0:T(8,128)(2,1)S(1)} %copy-done.22), channel_id=1, source_target_pairs={{0,127},{1,112},{2,113},{3,114},{4,115},{5,116},{6,117},{7,118},{8... | collective-permute-start | bytes 110600 | tf_op jit(solution)/shard_map/ppermute | solution.py:331
  79.6 6.8 %copy-start.9 = (bf16[1,144,128]{2,1,0:T(8,128)(2,1)}, bf16[1,144,128]{2,1,0:T(8,128)(2,1)S(1)}, u32[]{:S(2)}) copy-start(bf16[1,144,128]{2,1,0:T(8,128)(2,1)S(1)} %collective-permute-done.5.rest_5_) | copy-start | bytes 110596
  79.6 6.7 %collective-permute-start.2 = (bf16[4,144,128]{2,1,0:T(8,128)(2,1)S(1)}, bf16[4,144,128]{2,1,0:T(8,128)(2,1)S(1)}, u32[]{:S(2)}, u32[]{:S(2)}) collective-permute-start(bf16[4,144,128]{2,1,0:T(8,128)(2,1)S(1)} %copy-done.21), channel_id=1, source_target_pairs={{0,1},{1,2},{2,3},{3,4},{4,5},{5,6},{6,7},{7,8},{8,9},{9,10},{10,1... | collective-permute-start | bytes 442376 | tf_op jit(solution)/shard_map/ppermute | solution.py:331
  79.7 6.7 %copy-start.10 = (bf16[1,144,128]{2,1,0:T(8,128)(2,1)}, bf16[1,144,128]{2,1,0:T(8,128)(2,1)S(1)}, u32[]{:S(2)}) copy-start(bf16[1,144,128]{2,1,0:T(8,128)(2,1)S(1)} %collective-permute-done.6.rest_6_) | copy-start | bytes 110596
  79.7 6.6 %collective-permute-start.3 = (bf16[4,144,128]{2,1,0:T(8,128)(2,1)S(1)}, bf16[4,144,128]{2,1,0:T(8,128)(2,1)S(1)}, u32[]{:S(2)}, u32[]{:S(2)}) collective-permute-start(bf16[4,144,128]{2,1,0:T(8,128)(2,1)S(1)} %copy-done.20), channel_id=1, source_target_pairs={{0,15},{1,0},{2,1},{3,2},{4,3},{5,4},{6,5},{7,6},{8,7},{9,8},{10,9... | collective-permute-start | bytes 442376 | tf_op jit(solution)/shard_map/ppermute | solution.py:331
  84.9 1.5 copy-start.11
  86.3 0.7 copy-start.4
  86.3 0.7 copy-start.5
  86.4 0.8 copy-start
  86.4 0.9 copy-start.1
  129.0 59.3 %all-to-all-start = ((bf16[128,128,128]{2,1,0:T(8,128)(2,1)}), bf16[128,128,128]{2,1,0:T(8,128)(2,1)}, u32[]{:S(2)}, u32[]{:S(2)}) async-start(bf16[128,128,128]{2,1,0:T(8,128)(2,1)} %get-tuple-element.37), calls=%async_computation | async-start | bytes 8388608 | tf_op jit(solution)/shard_map/all_to_all | solution.py:335
  188.3 79.2 %all-to-all-start.2 = ((bf16[128,32,128]{2,1,0:T(8,128)(2,1)}), bf16[128,32,128]{2,1,0:T(8,128)(2,1)S(1)}, u32[]{:S(2)}, u32[]{:S(2)}) async-start(bf16[128,32,128]{2,1,0:T(8,128)(2,1)} %bitcast.8), calls=%async_computation.2 | async-start | bytes 2097152 | tf_op jit(solution)/shard_map/all_to_all | solution.py:335
  227.6 32.9 %collective-permute-start.8 = (bf16[8,128,128]{2,1,0:T(8,128)(2,1)}, bf16[8,128,128]{2,1,0:T(8,128)(2,1)S(1)}, u32[]{:S(2)}, u32[]{:S(2)}) collective-permute-start(bf16[8,128,128]{2,1,0:T(8,128)(2,1)} %get-tuple-element.44), channel_id=1, source_target_pairs={{0,16},{1,17},{2,18},{3,19},{4,20},{5,21},{6,22},{7,23},{8,24},{9,... | collective-permute-start | bytes 786440 | tf_op jit(solution)/shard_map/ppermute | solution.py:331
  228.7 31.9 %collective-permute-start.9 = (bf16[8,128,128]{2,1,0:T(8,128)(2,1)}, bf16[8,128,128]{2,1,0:T(8,128)(2,1)S(1)}, u32[]{:S(2)}, u32[]{:S(2)}) collective-permute-start(bf16[8,128,128]{2,1,0:T(8,128)(2,1)} %get-tuple-element.45), channel_id=1, source_target_pairs={{0,112},{1,113},{2,114},{3,115},{4,116},{5,117},{6,118},{7,119},{8... | collective-permute-start | bytes 786440 | tf_op jit(solution)/shard_map/ppermute | solution.py:331
  233.4 9.5 %collective-permute-start.12 = (bf16[1,128,128]{2,1,0:T(8,128)(2,1)}, bf16[1,128,128]{2,1,0:T(8,128)(2,1)S(1)}, u32[]{:S(2)}, u32[]{:S(2)}) collective-permute-start(bf16[1,128,128]{2,1,0:T(8,128)(2,1)} %get-tuple-element.48), channel_id=1, source_target_pairs={{0,17},{1,18},{2,19},{3,20},{4,21},{5,22},{6,23},{7,24},{8,25},{9,... | collective-permute-start | bytes 98312 | tf_op jit(solution)/shard_map/ppermute | solution.py:331
  233.4 27.2 %collective-permute-start.10 = (bf16[4,128,128]{2,1,0:T(8,128)(2,1)}, bf16[4,128,128]{2,1,0:T(8,128)(2,1)S(1)}, u32[]{:S(2)}, u32[]{:S(2)}) collective-permute-start(bf16[4,128,128]{2,1,0:T(8,128)(2,1)} %get-tuple-element.46), channel_id=1, source_target_pairs={{0,1},{1,2},{2,3},{3,4},{4,5},{5,6},{6,7},{7,8},{8,9},{9,10},{10,1... | collective-permute-start | bytes 393224 | tf_op jit(solution)/shard_map/ppermute | solution.py:331
  233.4 27.2 %collective-permute-start.11 = (bf16[4,128,128]{2,1,0:T(8,128)(2,1)}, bf16[4,128,128]{2,1,0:T(8,128)(2,1)S(1)}, u32[]{:S(2)}, u32[]{:S(2)}) collective-permute-start(bf16[4,128,128]{2,1,0:T(8,128)(2,1)} %get-tuple-element.47), channel_id=1, source_target_pairs={{0,15},{1,0},{2,1},{3,2},{4,3},{5,4},{6,5},{7,6},{8,7},{9,8},{10,9... | collective-permute-start | bytes 393224 | tf_op jit(solution)/shard_map/ppermute | solution.py:331
  242.8 17.8 %copy-start.12 = (bf16[1,128,128]{2,1,0:T(8,128)(2,1)}, bf16[1,128,128]{2,1,0:T(8,128)(2,1)S(1)}, u32[]{:S(2)}) copy-start(bf16[1,128,128]{2,1,0:T(8,128)(2,1)S(1)} %collective-permute-done.12.rest_4_) | copy-start | bytes 98308
  242.8 7.2 %collective-permute-start.13 = (bf16[1,128,128]{2,1,0:T(8,128)(2,1)}, bf16[1,128,128]{2,1,0:T(8,128)(2,1)S(1)}, u32[]{:S(2)}, u32[]{:S(2)}) collective-permute-start(bf16[1,128,128]{2,1,0:T(8,128)(2,1)} %get-tuple-element.49), channel_id=1, source_target_pairs={{0,31},{1,16},{2,17},{3,18},{4,19},{5,20},{6,21},{7,22},{8,23},{9,... | collective-permute-start | bytes 98312 | tf_op jit(solution)/shard_map/ppermute | solution.py:331
  250.0 10.6 %copy-start.13 = (bf16[1,128,128]{2,1,0:T(8,128)(2,1)}, bf16[1,128,128]{2,1,0:T(8,128)(2,1)S(1)}, u32[]{:S(2)}) copy-start(bf16[1,128,128]{2,1,0:T(8,128)(2,1)S(1)} %collective-permute-done.13.rest_5_) | copy-start | bytes 98308
  250.0 6.6 %collective-permute-start.14 = (bf16[1,128,128]{2,1,0:T(8,128)(2,1)}, bf16[1,128,128]{2,1,0:T(8,128)(2,1)S(1)}, u32[]{:S(2)}, u32[]{:S(2)}) collective-permute-start(bf16[1,128,128]{2,1,0:T(8,128)(2,1)} %get-tuple-element.50), channel_id=1, source_target_pairs={{0,113},{1,114},{2,115},{3,116},{4,117},{5,118},{6,119},{7,120},{8... | collective-permute-start | bytes 98312 | tf_op jit(solution)/shard_map/ppermute | solution.py:331
  256.6 4.1 %copy-start.14 = (bf16[1,128,128]{2,1,0:T(8,128)(2,1)}, bf16[1,128,128]{2,1,0:T(8,128)(2,1)S(1)}, u32[]{:S(2)}) copy-start(bf16[1,128,128]{2,1,0:T(8,128)(2,1)S(1)} %collective-permute-done.14.rest_6_) | copy-start | bytes 98308
  256.6 4.0 %collective-permute-start.15 = (bf16[1,128,128]{2,1,0:T(8,128)(2,1)}, bf16[1,128,128]{2,1,0:T(8,128)(2,1)S(1)}, u32[]{:S(2)}, u32[]{:S(2)}) collective-permute-start(bf16[1,128,128]{2,1,0:T(8,128)(2,1)} %get-tuple-element.51), channel_id=1, source_target_pairs={{0,127},{1,112},{2,113},{3,114},{4,115},{5,116},{6,117},{7,118},{8... | collective-permute-start | bytes 98312 | tf_op jit(solution)/shard_map/ppermute | solution.py:331
  260.6 0.6 copy-start.15
  260.6 0.7 copy-start.6
  260.6 0.7 copy-start.7
  260.6 0.8 copy-start.2
  260.6 0.8 copy-start.3

commit v2 on v1

v2 whole, which is shorter than its diff:
```python
import functools
import math

import jax
import jax.numpy as jnp
from jax import lax
from jax.experimental import pallas as pl
from jax.experimental.pallas import tpu as pltpu
from jax.sharding import PartitionSpec as P


AXES = ("gx", "gy")
SHARPNESS = 2.0
FAR = 9984.0
POS_ROWS = 16
BLOCK = 4
TILE = 16
VMEM_LIMIT = 60 * 1024 * 1024

f32 = jnp.float32
bf16 = jnp.bfloat16

SIDES = 4
STEPS = ((1, 0), (-1, 0), (0, 1), (0, -1), (1, 1), (1, -1), (-1, 1), (-1, -1))


def picks(step, grid, low, span):
    if step == 0:
        return list(range(low, low + span))
    return [grid[1]] if step > 0 else [grid[0]]


def border(step, rows, cols):
    return [
        (r, c)
        for r in picks(step[0], (0, rows - 1), 0, rows)
        for c in picks(step[1], (0, cols - 1), 0, cols)
    ]


def rim(step, rows, cols):
    return [
        (r, c)
        for r in picks(step[0], (0, rows + 1), 1, rows)
        for c in picks(step[1], (0, cols + 1), 1, cols)
    ]


def vmem(*_):
    return pl.BlockSpec(memory_space=pltpu.VMEM)


def hbm(*_):
    return pl.BlockSpec(memory_space=pl.ANY)


def smem(*_):
    return pl.BlockSpec(memory_space=pltpu.SMEM)


def params(**extra):
    return pltpu.CompilerParams(vmem_limit_bytes=VMEM_LIMIT, **extra)


def pack_kernel(dims, counts, slots, features, positions, cotangent, *rest):
    rows, cols, slot_count = dims
    leaves = rows * cols
    home, *sends = rest[: SIDES + 1]
    packed, sem = rest[SIDES + 1 :]
    copies = [
        pltpu.make_async_copy(cotangent.at[g], packed.at[slots[g] // leaves], sem.at[g])
        for g in range(leaves)
    ]
    for copy in copies:
        copy.start()
    lane = lax.broadcasted_iota(jnp.int32, (1, slot_count), 1)
    pad = jnp.zeros((POS_ROWS - 3, slot_count), f32)
    for r in range(rows):
        place = [positions[r, axis].astype(f32) for axis in range(3)]
        for c in range(cols):
            leaf = r * cols + c
            x = jnp.where(lane < counts[r, c], place[0][c : c + 1], FAR)
            block = jnp.concatenate([x, place[1][c : c + 1], place[2][c : c + 1], pad], axis=0)
            home[leaf, slot_count:, :] = block.astype(bf16)
    home[:, :slot_count, :] = features[...]
    for step, send in zip(STEPS, sends):
        for index, (r, c) in enumerate(border(step, rows, cols)):
            send[index] = home[r * cols + c]
    for copy in copies:
        copy.wait()


def forward_kernel(dims, codes, counts, slots, home, *rest):
    rows, cols, slot_count, channels, radial, neigh = dims
    halos = rest[: SIDES + 2]
    bins_ref, weights = rest[SIDES + 2 : SIDES + 4]
    slope, coupling_out, gathered, packed = rest[SIDES + 4 : SIDES + 8]
    ghost, turned, weights_t, outgoing, sem_in, sem_out = rest[SIDES + 8 :]
    block = pl.program_id(0)
    wide = cols + 2
    leaves = rows * cols

    @pl.when(block == 0)
    def _():
        copies = []
        for r in range(rows):
            copies.append((home.at[pl.ds(r * cols, cols)], ghost.at[pl.ds((r + 1) * wide + 1, cols)]))
        spots = [rim((-step[0], -step[1]), rows, cols) for step in STEPS[:SIDES]]
        spots += [[(0, c), (rows + 1, c)] for c in (0, cols + 1)]
        for spot, halo in zip(spots, halos):
            if len(spot) == cols:
                copies.append((halo, ghost.at[pl.ds(spot[0][0] * wide + spot[0][1], cols)]))
            else:
                for index, (r, c) in enumerate(spot):
                    copies.append((halo.at[index], ghost.at[r * wide + c]))
        copies = [
            pltpu.make_async_copy(source, target, sem_in.at[index])
            for index, (source, target) in enumerate(copies)
        ]
        for copy in copies:
            copy.start()
        for k in range(radial):
            weights_t[:, k * channels : (k + 1) * channels] = weights[
                k * channels : (k + 1) * channels, :
            ].T
        for copy in copies:
            copy.wait()

        def turn(leaf, carry):
            turned[leaf] = ghost[leaf, pl.ds(0, slot_count), :].T
            return carry

        lax.fori_loop(0, (rows + 2) * wide, turn, 0, unroll=4)

    row_index = lax.broadcasted_iota(jnp.int32, (slot_count, slot_count), 0)
    col_index = lax.broadcasted_iota(jnp.int32, (slot_count, slot_count), 1)
    lane = lax.broadcasted_iota(jnp.int32, (channels, slot_count), 1)

    def place_of(leaf):
        return leaf // cols, leaf % cols

    def build(index):
        leaf = block * BLOCK + index
        r, c = place_of(leaf)
        own = (r + 1) * wide + c + 1
        place = ghost[own, pl.ds(slot_count, POS_ROWS), :].astype(f32)
        columns = place[:8].T
        receiver = [
            jnp.broadcast_to(columns[:, axis : axis + 1], (slot_count, slot_count))
            for axis in range(3)
        ]
        bins = bins_ref[leaf]
        tiles = []
        for n in range(neigh):
            code = codes[r, n, c]
            row_off = code // 3
            col_off = code % 3
            sender = (r + row_off) * wide + c + col_off
            remote = ghost[sender, pl.ds(slot_count, POS_ROWS), :].astype(f32)
            delta_x = (remote[0:1] + (row_off - 1).astype(f32)) - receiver[0]
            delta_y = (remote[1:2] + (col_off - 1).astype(f32)) - receiver[1]
            delta_z = remote[2:3] - receiver[2]
            distance = delta_x * delta_x + delta_y * delta_y + delta_z * delta_z
            coupling = jnp.exp(-SHARPNESS * distance)
            if n == 0:
                coupling = jnp.where(row_index == col_index, 0.0, coupling)
            coupling = coupling.astype(bf16)
            coupling_out[index * neigh + n] = coupling
            tiles.append(
                lax.dot_general(
                    turned[sender],
                    coupling,
                    (((1,), (1,)), ((), ())),
                    preferred_element_type=f32,
                )
            )
        merged = []
        for n in range(neigh):
            total = tiles[n]
            for m in range(n):
                same = jnp.broadcast_to(bins[m : m + 1] == bins[n : n + 1], total.shape)
                total = total + jnp.where(same, tiles[m], 0.0)
            merged.append(total.astype(bf16))
        marks = bin_marks(bins)
        for k in range(radial):
            masks = [mark == jnp.bfloat16(k) for mark in marks]
            for part in range(channels // TILE):
                value = jnp.zeros((TILE, slot_count), bf16)
                for n in range(neigh):
                    value = jnp.where(
                        masks[n], merged[n][part * TILE : (part + 1) * TILE], value
                    )
                first = k * channels + part * TILE
                gathered[index, first : first + TILE, :] = value

    def sends(at):
        copies = []
        for index in range(BLOCK):
            r, c = place_of(at * BLOCK + index)
            copies.append(
                pltpu.make_async_copy(
                    outgoing.at[index], packed.at[slots[r, c] // leaves], sem_out.at[index]
                )
            )
        return copies

    @pl.when(block > 0)
    def _():
        for copy in sends(block - 1):
            copy.wait()

    for pair in range(BLOCK // 2):
        for index in (2 * pair, 2 * pair + 1):
            build(index)
        message = jnp.dot(
            weights_t[...],
            jnp.concatenate([gathered[2 * pair], gathered[2 * pair + 1]], axis=1),
            preferred_element_type=f32,
        )
        for side in range(2):
            index = 2 * pair + side
            r, c = place_of(block * BLOCK + index)
            value = message[:, side * slot_count : (side + 1) * slot_count]
            valid = (lane < counts[r, c]).astype(f32)
            logistic = 1.0 / (1.0 + jnp.exp(-value))
            outgoing[index] = (value * logistic * valid).T.astype(bf16)
            slope[:, index * slot_count : (index + 1) * slot_count] = (
                valid * logistic * (1.0 + value * (1.0 - logistic))
            )
    for copy in sends(block):
        copy.start()

    @pl.when(block == pl.num_programs(0) - 1)
    def _():
        for copy in sends(block):
            copy.wait()


def bin_marks(bins):
    return [
        jnp.broadcast_to(bins[n : n + 1].astype(f32), (TILE, bins.shape[1])).astype(bf16)
        for n in range(bins.shape[0])
    ]


def backward_kernel(
    dims, scale, codes, slots, slope, coupling, gathered, bins_ref, weights, returned, *rest
):
    rows, cols, slot_count, channels, radial, neigh = dims
    own, grad = rest[:2]
    sends = rest[2:10]
    padded, full_a, full_b, total, home_grad, grads_a, grads_b, sem = rest[10:]
    width = radial * channels
    block = pl.program_id(0)
    wide = cols + 2
    leaves = rows * cols

    @pl.when(block == 0)
    def _():
        copies = [
            pltpu.make_async_copy(
                returned.at[slots[leaf // cols, leaf % cols] // leaves],
                home_grad.at[leaf],
                sem.at[leaf],
            )
            for leaf in range(leaves)
        ]
        for copy in copies:
            copy.start()
        padded[...] = jnp.zeros_like(padded)
        total[...] = jnp.zeros_like(total)
        for copy in copies:
            copy.wait()

    span = width // BLOCK

    def prepare(at, grads):
        for index in range(BLOCK):
            leaf = at * BLOCK + index
            low = index * slot_count
            first = pl.multiple_of(leaf * slot_count, slot_count)
            grads[:, low : low + slot_count] = (
                home_grad[leaf].astype(f32).T * slope[:, pl.ds(first, slot_count)]
            ).astype(bf16)

    chunks = 8
    rows_each = span // chunks

    def expand(index, chunk, grads, full):
        first = pl.multiple_of(index * span + chunk * rows_each, rows_each)
        product = jnp.dot(
            weights[pl.ds(first, rows_each), :], grads[...], preferred_element_type=f32
        ).astype(bf16)
        for leaf in range(BLOCK):
            full[leaf, pl.ds(first, rows_each), :] = product[
                :, leaf * slot_count : (leaf + 1) * slot_count
            ]

    def collect_weight(index, chunk, grads):
        low = 2 * chunk * rows_each
        first = pl.multiple_of(index * span + low, rows_each)
        total[index, :, low : low + 2 * rows_each] += lax.dot_general(
            grads[...],
            jnp.concatenate(
                [gathered[leaf, pl.ds(first, 2 * rows_each), :] for leaf in range(BLOCK)], axis=1
            ),
            (((1,), (1,)), ((), ())),
            preferred_element_type=f32,
        )

    def work(now, later):
        grads, full = now
        grads_later, full_later = later
        prepare(jnp.minimum(block + 1, pl.num_programs(0) - 1), grads_later)
        per_half = channels // TILE // 2
        bins_each = 2 * radial // chunks

        def leaf_step(index, carry):
            leaf = block * BLOCK + index
            r = leaf // cols
            c = leaf % cols
            marks = bin_marks(bins_ref[leaf])
            halves = [[] for _ in range(neigh)]
            for half in range(2):
                spots = [(half * per_half + part) * TILE for part in range(per_half)]
                values = [[jnp.zeros((TILE, slot_count), bf16)] * per_half for _ in range(neigh)]
                for quarter in range(chunks // 2):
                    chunk = half * (chunks // 2) + quarter
                    expand(index, chunk, grads_later, full_later)
                    if chunk % 2 == 0:
                        collect_weight(index, chunk // 2, grads)
                    for k in range(quarter * bins_each, (quarter + 1) * bins_each):
                        masks = [mark == jnp.bfloat16(k) for mark in marks]
                        for part, spot in enumerate(spots):
                            first = k * channels + spot
                            row = full[index, first : first + TILE, :]
                            for n in range(neigh):
                                values[n][part] = jnp.where(masks[n], row, values[n][part])
                for n in range(neigh):
                    halves[n].extend(values[n])
            for n in range(neigh):
                code = codes[r, n, c]
                sender = (r + code // 3) * wide + c + code % 3
                padded[sender] += jnp.dot(
                    jnp.concatenate(halves[n], axis=0),
                    coupling[index * neigh + n],
                    preferred_element_type=f32,
                )
            return carry

        lax.fori_loop(0, BLOCK, leaf_step, 0)

    first_set, second_set = (grads_a, full_a), (grads_b, full_b)

    @pl.when(block == 0)
    def _():
        prepare(block, grads_a)

        def first_step(index, carry):
            for chunk in range(chunks):
                expand(index, chunk, grads_a, full_a)
            return carry

        lax.fori_loop(0, BLOCK, first_step, 0)

    @pl.when(block % 2 == 0)
    def _():
        work(first_set, second_set)

    @pl.when(block % 2 == 1)
    def _():
        work(second_set, first_set)

    @pl.when(block == pl.num_programs(0) - 1)
    def _():
        for r in range(rows):
            first = (r + 1) * wide + 1
            own[r * cols : (r + 1) * cols] = padded[first : first + cols]
        for step, send in zip(STEPS, sends):
            for index, (r, c) in enumerate(rim(step, rows, cols)):
                send[index] = padded[r * wide + c].astype(send.dtype)
        per_span = span // channels
        for k in range(radial):
            low = k % per_span * channels
            grad[k * channels : (k + 1) * channels, :] = (
                total[k // per_span, :, low : low + channels].T * scale
            ).astype(grad.dtype)


def fold_kernel(dims, own, *rest):
    rows, cols = dims
    received = rest[:8]
    out, total = rest[8:]
    total[...] = own[...]
    for step, piece in zip(STEPS, received):
        for index, (r, c) in enumerate(border((-step[0], -step[1]), rows, cols)):
            total[r * cols + c] += piece[index].astype(f32)
    for leaf in range(rows * cols):
        out[leaf] = total[leaf].T.astype(bf16)


def collect_kernel(leaves, slots, arrived, out, sem):
    copies = [
        pltpu.make_async_copy(arrived.at[slots[g] // leaves], out.at[g], sem.at[g])
        for g in range(leaves)
    ]
    for copy in copies:
        copy.start()
    for copy in copies:
        copy.wait()


def shift(value, step, shape):
    gx, gy = shape
    pairs = [
        (i * gy + j, (i + step[0]) % gx * gy + (j + step[1]) % gy)
        for i in range(gx)
        for j in range(gy)
    ]
    return lax.ppermute(value, AXES, pairs)


def relay(buffer):
    return lax.all_to_all(buffer, AXES, split_axis=0, concat_axis=0, tiled=True)


def shards(
    features,
    positions,
    neighbours,
    atom_counts,
    radial_bins,
    destination,
    anchor,
    weights,
    cotangent,
):
    rows, cols, slot_count, channels = features.shape
    neigh = neighbours.shape[2]
    radial = weights.shape[0]
    leaves = rows * cols
    shape = (lax.axis_size("gx"), lax.axis_size("gy"))
    peers = shape[0] * shape[1]
    padded = (rows + 2) * (cols + 2)
    blocks = leaves // BLOCK
    tall = slot_count + POS_ROWS
    width = radial * channels
    any_dma = pltpu.SemaphoreType.DMA

    codes = neighbours.transpose(0, 2, 1)
    bins = radial_bins.reshape(leaves, neigh, slot_count)
    weight_rows = weights.reshape(width, channels)
    sizes = [len(border(step, rows, cols)) for step in STEPS]

    home, *rest = pl.pallas_call(
        functools.partial(pack_kernel, (rows, cols, slot_count)),
        out_shape=[jax.ShapeDtypeStruct((leaves, tall, channels), bf16)]
        + [jax.ShapeDtypeStruct((size, tall, channels), bf16) for size in sizes[:SIDES]]
        + [jax.ShapeDtypeStruct((peers, slot_count, channels), bf16)],
        in_specs=[smem(), smem(), vmem(), vmem(), vmem()],
        out_specs=[vmem()] * (SIDES + 1) + [hbm()],
        scratch_shapes=[any_dma((leaves,))],
        compiler_params=params(),
        name="pack",
    )(
        atom_counts,
        anchor,
        features.reshape(leaves, slot_count, channels),
        positions.transpose(0, 2, 1, 3),
        cotangent,
    )
    sends, cot_packed = rest[:SIDES], rest[SIDES]
    halos = []
    for send, step in zip(sends, STEPS):
        halos.append(shift(send, step, shape))
    low, high = halos[:2]
    for step, at in (((0, 1), cols - 1), ((0, -1), 0)):
        corners = jnp.concatenate([low[at : at + 1], high[at : at + 1]], axis=0)
        halos.append(shift(corners, step, shape))
    returned = relay(cot_packed)

    slope, coupling, gathered, packed = pl.pallas_call(
        functools.partial(forward_kernel, (rows, cols, slot_count, channels, radial, neigh)),
        grid=(blocks,),
        out_shape=[
            jax.ShapeDtypeStruct((channels, leaves * slot_count), f32),
            jax.ShapeDtypeStruct((leaves * neigh, slot_count, slot_count), bf16),
            jax.ShapeDtypeStruct((leaves, width, slot_count), bf16),
            jax.ShapeDtypeStruct((peers, slot_count, channels), bf16),
        ],
        in_specs=[smem(), smem(), smem(), hbm()] + [hbm()] * (SIDES + 2) + [vmem(), vmem()],
        out_specs=[
            pl.BlockSpec((channels, BLOCK * slot_count), lambda b: (0, b)),
            pl.BlockSpec((BLOCK * neigh, slot_count, slot_count), lambda b: (b, 0, 0)),
            pl.BlockSpec((BLOCK, width, slot_count), lambda b: (b, 0, 0)),
            hbm(),
        ],
        scratch_shapes=[
            pltpu.VMEM((padded, tall, channels), bf16),
            pltpu.VMEM((padded, channels, slot_count), bf16),
            pltpu.VMEM((channels, width), bf16),
            pltpu.VMEM((BLOCK, slot_count, channels), bf16),
            any_dma((2 * (rows + cols) + rows + 8,)),
            any_dma((BLOCK,)),
        ],
        compiler_params=params(dimension_semantics=("arbitrary",)),
        name="forward",
    )(codes, atom_counts, destination, home, *halos, bins, weight_rows)

    arrived = relay(packed)

    grad_scale = 1.0 / math.sqrt(peers * leaves * slot_count)
    own, weight_part, *grad_sends = pl.pallas_call(
        functools.partial(
            backward_kernel, (rows, cols, slot_count, channels, radial, neigh), grad_scale
        ),
        grid=(blocks,),
        out_shape=[
            jax.ShapeDtypeStruct((leaves, channels, slot_count), f32),
            jax.ShapeDtypeStruct((width, channels), bf16),
        ]
        + [jax.ShapeDtypeStruct((size, channels, slot_count), bf16) for size in sizes],
        in_specs=[
            smem(),
            smem(),
            vmem(),
            pl.BlockSpec((BLOCK * neigh, slot_count, slot_count), lambda b: (b, 0, 0)),
            pl.BlockSpec((BLOCK, width, slot_count), lambda b: (b, 0, 0)),
            vmem(),
            vmem(),
            hbm(),
        ],
        out_specs=[vmem()] * 10,
        scratch_shapes=[
            pltpu.VMEM((padded, channels, slot_count), f32),
            pltpu.VMEM((BLOCK, width, slot_count), bf16),
            pltpu.VMEM((BLOCK, width, slot_count), bf16),
            pltpu.VMEM((BLOCK, channels, width // BLOCK), f32),
            pltpu.VMEM((leaves, slot_count, channels), bf16),
            pltpu.VMEM((channels, BLOCK * slot_count), bf16),
            pltpu.VMEM((channels, BLOCK * slot_count), bf16),
            any_dma((leaves,)),
        ],
        compiler_params=params(dimension_semantics=("arbitrary",)),
        name="backward",
    )(codes, destination, slope, coupling, gathered, bins, weight_rows, returned)

    weight_pieces = relay(weight_part.reshape(peers, width // peers, channels))

    received = []
    for send, step in zip(grad_sends, STEPS):
        received.append(shift(send, step, shape))
    feature_grad = pl.pallas_call(
        functools.partial(fold_kernel, (rows, cols)),
        out_shape=jax.ShapeDtypeStruct((leaves, slot_count, channels), bf16),
        in_specs=[vmem()] * 9,
        out_specs=vmem(),
        scratch_shapes=[pltpu.VMEM((leaves, slot_count, channels), f32)],
        compiler_params=params(),
        name="fold",
    )(own, *received)

    updated = pl.pallas_call(
        functools.partial(collect_kernel, leaves),
        out_shape=jax.ShapeDtypeStruct((leaves, slot_count, channels), bf16),
        in_specs=[smem(), hbm()],
        out_specs=vmem(),
        scratch_shapes=[any_dma((leaves,))],
        compiler_params=params(),
        name="collect",
    )(anchor, arrived)

    weight_grad = jnp.sum(weight_pieces.astype(f32), axis=0)
    return updated, feature_grad.reshape(rows, cols, slot_count, channels), weight_grad


def solution(mesh):
    leaf = P("gx", "gy")
    placed = (leaf, leaf, leaf, leaf, leaf, leaf, P(AXES), P(), P(AXES))
    return jax.shard_map(
        shards,
        mesh=mesh,
        in_specs=placed,
        out_specs=(P(AXES), leaf, P(AXES)),
        check_vma=False,
    )
```

time: 271 us -> 232 us (0.86)
  waiting for transfers between devices: 105 us -> 83.5 us
  Pallas kernels: 103 us -> 84.3 us
  starting transfers between devices: 52.9 us -> 58.3 us
    all_to_all x3, waiting for transfers between devices: 34.6 us -> 13.5 us  [relay(): return lax.all_to_all(buffer, AXES, split_axis=0, concat_axis=0, tiled=True)]
    pallas_call x1 -> x0, Pallas kernels: 17.5 us -> none  [shards(): pl.pallas_call(functools.partial(weight_kernel, (leaves, slot_count, chan...]
    pallas_call x1, Pallas kernels: 41.7 us -> 35.1 us  [shards(): pl.pallas_call(functools.partial(forward_kernel, (rows, cols, slot_count,...]
    pallas_call x1, Pallas kernels: 33.8 us -> 38.7 us  [shards(): pl.pallas_call(functools.partial(backward_kernel, (rows, cols, slot_count...]
    ppermute x16 -> x14, starting transfers between devices: 28.6 us -> 33.3 us  [shift(): return lax.ppermute(value, AXES, pairs)]
    ppermute x16 -> x14, waiting for transfers between devices: 70.1 us -> 70 us  [shift(): return lax.ppermute(value, AXES, pairs)]
  transfers between devices with their start and end apart: 19 -> 17, of which waited for: 7 -> 7; matrix products, arithmetic and copies ran while one was open for 1% -> 0% of each run, Pallas kernels for 37% -> 35%
where the time goes in v2:
time: 232 us; the launch traced here: 229 us
  Pallas kernels  84.3 us (36%)
  waiting for transfers between devices  83.5 us (36%)
  starting transfers between devices  58.3 us (25%)
    ppermute x14, waiting for transfers between devices, shift(): return lax.ppermute(value, AXES, pairs)  70 us
    pallas_call x1, Pallas kernels, shards(): pl.pallas_call(functools.partial(backward_kernel, (rows, cols, slot_count...  38.7 us
    pallas_call x1, Pallas kernels, shards(): pl.pallas_call(functools.partial(forward_kernel, (rows, cols, slot_count,...  35.1 us
    ppermute x14, starting transfers between devices, shift(): return lax.ppermute(value, AXES, pairs)  33.3 us
    all_to_all x3, starting transfers between devices, relay(): return lax.all_to_all(buffer, AXES, split_axis=0, concat_axis=0, tiled=True)  25 us
    all_to_all x3, waiting for transfers between devices, relay(): return lax.all_to_all(buffer, AXES, split_axis=0, concat_axis=0, tiled=True)  13.5 us
  transfers between devices with their start and end apart: 17, of which 7 were waited for; matrix products, arithmetic and copies ran while one was open for 0% of the time, Pallas kernels for 35%

profile of v2, /device:TPU:0, one launch (start us, length us, event | category | flops | bytes accessed | tf_op | source)
XLA Modules:
  0.0 229.3 jit_solution(18178809397969894983)
XLA Ops:
  0.6 4.3 %pack.1 = (bf16[32,144,128]{2,1,0:T(8,128)(2,1)}, bf16[8,144,128]{2,1,0:T(8,128)(2,1)}, bf16[8,144,128]{2,1,0:T(8,128)(2,1)}, bf16[4,144,128]{2,1,0:T(8,128)(2,1...) custom-call(s32[4,8]{1,0:T(4,128)} %counts.3, s32[32]{0:T(128)} %slots.6, bf16[32,128,128]{2,1,0:T(8,128)(2,1)} %bitcast.9, ...), custom_call_target="tpu_custom_call" | custom-call | tf_op jit(solution)/shard_map/pack/pallas_call | solution.py:455
  4.9 0.0 copy-start.15
  5.0 0.0 copy-start.14
  5.0 0.0 copy-start.17
  5.0 0.0 copy-start.16
  5.0 11.7 %all-to-all-start.1 = ((bf16[128,128,128]{2,1,0:T(8,128)(2,1)}), bf16[128,128,128]{2,1,0:T(8,128)(2,1)}, u32[]{:S(2)}, u32[]{:S(2)}) async-start(bf16[128,128,128]{2,1,0:T(8,128)(2,1)} %get-tuple-element.32), calls=%async_computation.1 | async-start | bytes 8388608 | tf_op jit(solution)/shard_map/all_to_all | solution.py:424
  16.7 0.0 copy-done.15
  16.7 1.0 collective-permute-start
  17.7 0.0 copy-done.14
  17.7 4.8 %collective-permute-start.1 = (bf16[8,144,128]{2,1,0:T(8,128)(2,1)S(1)}, bf16[8,144,128]{2,1,0:T(8,128)(2,1)S(1)}, u32[]{:S(2)}, u32[]{:S(2)}) collective-permute-start(bf16[8,144,128]{2,1,0:T(8,128)(2,1)S(1)} %copy-done.14), channel_id=1, source_target_pairs={{0,112},{1,113},{2,114},{3,115},{4,116},{5,117},{6,118},{7,119},{8... | collective-permute-start | bytes 884744 | tf_op jit(solution)/shard_map/ppermute | solution.py:420
  22.4 0.0 copy-done.17
  22.4 0.0 collective-permute-start.2
  22.4 0.0 copy-done.16
  22.4 3.9 %collective-permute-start.3 = (bf16[4,144,128]{2,1,0:T(8,128)(2,1)S(1)}, bf16[4,144,128]{2,1,0:T(8,128)(2,1)S(1)}, u32[]{:S(2)}, u32[]{:S(2)}) collective-permute-start(bf16[4,144,128]{2,1,0:T(8,128)(2,1)S(1)} %copy-done.16), channel_id=1, source_target_pairs={{0,15},{1,0},{2,1},{3,2},{4,3},{5,4},{6,5},{7,6},{8,7},{9,8},{10,9... | collective-permute-start | bytes 442376 | tf_op jit(solution)/shard_map/ppermute | solution.py:420
  26.3 46.1 %collective-permute-done.rest_0_ = bf16[8,144,128]{2,1,0:T(8,128)(2,1)S(1)} collective-permute-done((bf16[8,144,128]{2,1,0:T(8,128)(2,1)S(1)}, bf16[8,144,128]{2,1,0:T(8,128)(2,1)S(1)}, u32[]{:S(2)}, u32[]{:S(2)}) %collective-permute-start) | collective-permute-done | bytes 294944 | tf_op jit(solution)/shard_map/ppermute | solution.py:420
  72.4 0.0 collective-permute-done.1.rest_1_
  72.4 0.0 copy-start.1
  72.5 0.1 collective-permute-start.4
  72.6 3.9 %collective-permute-start.5 = (bf16[2,144,128]{2,1,0:T(8,128)(2,1)S(1)}, bf16[2,144,128]{2,1,0:T(8,128)(2,1)S(1)}, u32[]{:S(2)}, u32[]{:S(2)}) collective-permute-start(bf16[2,144,128]{2,1,0:T(8,128)(2,1)S(1)} %pad_maximum_fusion.1), channel_id=1, source_target_pairs={{0,15},{1,0},{2,1},{3,2},{4,3},{5,4},{6,5},{7,6},{8,7},{9,8},{10,9... | collective-permute-start | bytes 221192 | tf_op jit(solution)/shard_map/ppermute | solution.py:420
  76.5 0.0 collective-permute-done.2.rest_2_
  76.5 0.0 collective-permute-done.3.rest_3_
  76.5 0.0 copy-start.5
  76.5 1.9 collective-permute-done.4.rest_4_
  78.4 0.0 collective-permute-done.5.rest_5_
  78.5 0.0 copy-done
  78.5 0.0 copy-done.1
  78.5 0.0 copy-done.4
  78.5 0.0 copy-done.5
  78.5 0.6 copy-done.8
  79.1 0.0 copy-done.9
  79.1 35.1 %forward.1 = (f32[128,4096]{1,0:T(8,128)}, bf16[128,128,128]{2,1,0:T(8,128)(2,1)}, bf16[32,4096,128]{2,1,0:T(8,128)(2,1)}, bf16[128,128,128]{2,1,0:T(8,128)(2,1)}) custom-call(s32[4,4,8]{2,1,0:T(4,128)} %bitcast.14, s32[4,8]{1,0:T(4,128)} %counts.3, s32[4,8]{1,0:T(4,128)} %slots.7, bf16[32,144,128]{2,1,0:T(8,128)(2,1)} %get-tuple-element.23.home, ...), custom_call_target="tpu_custom_call" | custom-call | tf_op jit(solution)/shard_map/forward/pallas_call | solution.py:482
  114.2 0.0 all-to-all-done.1.returned
  114.2 7.9 %all-to-all-start = ((bf16[128,128,128]{2,1,0:T(8,128)(2,1)}), bf16[128,128,128]{2,1,0:T(8,128)(2,1)}, u32[]{:S(2)}, u32[]{:S(2)}) async-start(bf16[128,128,128]{2,1,0:T(8,128)(2,1)} %get-tuple-element.28), calls=%async_computation | async-start | bytes 8388608 | tf_op jit(solution)/shard_map/all_to_all | solution.py:424
  122.1 38.7 %backward.1 = (f32[32,128,128]{2,1,0:T(8,128)}, bf16[4096,128]{1,0:T(8,128)(2,1)}, bf16[8,128,128]{2,1,0:T(8,128)(2,1)}, bf16[8,128,128]{2,1,0:T(8,128)(2,1)}, b...) custom-call(s32[4,4,8]{2,1,0:T(4,128)} %bitcast.15, ...), custom_call_target="tpu_custom_call" | custom-call | tf_op jit(solution)/shard_map/backward/pallas_call | solution.py:513
  160.8 13.5 %all-to-all-done.arrived = bf16[128,128,128]{2,1,0:T(8,128)(2,1)} async-done(((bf16[128,128,128]{2,1,0:T(8,128)(2,1)}), bf16[128,128,128]{2,1,0:T(8,128)(2,1)}, u32[]{:S(2)}, u32[]{:S(2)}) %all-to-all-start) | async-done | bytes 4194336 | tf_op jit(solution)/shard_map/all_to_all | solution.py:424
  174.2 5.5 %all-to-all-start.2 = ((bf16[128,32,128]{2,1,0:T(8,128)(2,1)}), bf16[128,32,128]{2,1,0:T(8,128)(2,1)S(1)}, u32[]{:S(2)}, u32[]{:S(2)}) async-start(bf16[128,32,128]{2,1,0:T(8,128)(2,1)} %bitcast.10), calls=%async_computation.2 | async-start | bytes 2097152 | tf_op jit(solution)/shard_map/all_to_all | solution.py:424
  179.7 1.0 collective-permute-start.6
  180.7 4.7 %collective-permute-start.7 = (bf16[8,128,128]{2,1,0:T(8,128)(2,1)}, bf16[8,128,128]{2,1,0:T(8,128)(2,1)S(1)}, u32[]{:S(2)}, u32[]{:S(2)}) collective-permute-start(bf16[8,128,128]{2,1,0:T(8,128)(2,1)} %get-tuple-element.35), channel_id=1, source_target_pairs={{0,112},{1,113},{2,114},{3,115},{4,116},{5,117},{6,118},{7,119},{8... | collective-permute-start | bytes 786440 | tf_op jit(solution)/shard_map/ppermute | solution.py:420
  185.4 0.0 collective-permute-start.10
  185.4 0.0 collective-permute-start.8
  185.4 3.9 %collective-permute-start.9 = (bf16[4,128,128]{2,1,0:T(8,128)(2,1)}, bf16[4,128,128]{2,1,0:T(8,128)(2,1)S(1)}, u32[]{:S(2)}, u32[]{:S(2)}) collective-permute-start(bf16[4,128,128]{2,1,0:T(8,128)(2,1)} %get-tuple-element.37), channel_id=1, source_target_pairs={{0,15},{1,0},{2,1},{3,2},{4,3},{5,4},{6,5},{7,6},{8,7},{9,8},{10,9... | collective-permute-start | bytes 393224 | tf_op jit(solution)/shard_map/ppermute | solution.py:420
  189.3 10.1 %collective-permute-done.10.rest_4_ = bf16[1,128,128]{2,1,0:T(8,128)(2,1)S(1)} collective-permute-done((bf16[1,128,128]{2,1,0:T(8,128)(2,1)}, bf16[1,128,128]{2,1,0:T(8,128)(2,1)S(1)}, u32[]{:S(2)}, u32[]{:S(2)}) %collective-permute-start.10) | collective-permute-done | bytes 32800 | tf_op jit(solution)/shard_map/ppermute | solution.py:420
  199.3 3.2 %collective-permute-start.11 = (bf16[1,128,128]{2,1,0:T(8,128)(2,1)}, bf16[1,128,128]{2,1,0:T(8,128)(2,1)S(1)}, u32[]{:S(2)}, u32[]{:S(2)}) collective-permute-start(bf16[1,128,128]{2,1,0:T(8,128)(2,1)} %get-tuple-element.39), channel_id=1, source_target_pairs={{0,31},{1,16},{2,17},{3,18},{4,19},{5,20},{6,21},{7,22},{8,23},{9,... | collective-permute-start | bytes 98312 | tf_op jit(solution)/shard_map/ppermute | solution.py:420
  202.5 4.0 %collective-permute-done.11.rest_5_ = bf16[1,128,128]{2,1,0:T(8,128)(2,1)S(1)} collective-permute-done((bf16[1,128,128]{2,1,0:T(8,128)(2,1)}, bf16[1,128,128]{2,1,0:T(8,128)(2,1)S(1)}, u32[]{:S(2)}, u32[]{:S(2)}) %collective-permute-start.11) | collective-permute-done | bytes 32800 | tf_op jit(solution)/shard_map/ppermute | solution.py:420
  206.5 0.6 collective-permute-start.12
  207.1 5.9 %collective-permute-done.12.rest_6_ = bf16[1,128,128]{2,1,0:T(8,128)(2,1)S(1)} collective-permute-done((bf16[1,128,128]{2,1,0:T(8,128)(2,1)}, bf16[1,128,128]{2,1,0:T(8,128)(2,1)S(1)}, u32[]{:S(2)}, u32[]{:S(2)}) %collective-permute-start.12) | collective-permute-done | bytes 32800 | tf_op jit(solution)/shard_map/ppermute | solution.py:420
  213.1 6.4 %collective-permute-start.13 = (bf16[1,128,128]{2,1,0:T(8,128)(2,1)}, bf16[1,128,128]{2,1,0:T(8,128)(2,1)S(1)}, u32[]{:S(2)}, u32[]{:S(2)}) collective-permute-start(bf16[1,128,128]{2,1,0:T(8,128)(2,1)} %get-tuple-element.41), channel_id=1, source_target_pairs={{0,127},{1,112},{2,113},{3,114},{4,115},{5,116},{6,117},{7,118},{8... | collective-permute-start | bytes 98312 | tf_op jit(solution)/shard_map/ppermute | solution.py:420
  219.4 1.9 collective-permute-done.13.rest_7_
  221.3 0.0 collective-permute-done.8.rest_2_
  221.3 0.0 collective-permute-done.9.rest_3_
  221.3 0.0 copy-start.7
  221.4 0.0 collective-permute-done.6.rest_0_
  221.4 0.0 copy-start.2
  221.4 0.0 collective-permute-done.7.rest_1_
  221.4 0.0 copy-start.3
  221.4 0.5 copy-done.13
  221.9 0.1 copy-done.6
  222.0 0.1 copy-done.7
  222.1 0.1 copy-done.2
  222.1 0.1 copy-done.3
  222.2 3.1 %fold.1 = bf16[32,128,128]{2,1,0:T(8,128)(2,1)} custom-call(f32[32,128,128]{2,1,0:T(8,128)} %get-tuple-element.33.own, bf16[8,128,128]{2,1,0:T(8,128)(2,1)} %copy-done.2, bf16[8,128,128]{2,1,0:T(8,128)(2,1)} %copy-done.3, bf16[4,128,128]{2,1,0:T(8,128)(2,1)} %copy-done.6, bf16[4,128,128]{2,1,0:T(8,128)(2,1)} %copy-done.7, bf16[1,128,128]{2,1,0:T(8,128)(2,1)} %copy-done.10, ...), custom_call_target="tpu_custom_call" | custom-call | tf_op jit(solution)/shard_map/fold/pallas_call | solution.py:553
  225.3 3.1 %collect.1 = bf16[32,128,128]{2,1,0:T(8,128)(2,1)} custom-call(s32[32]{0:T(128)} %slots.6, bf16[128,128,128]{2,1,0:T(8,128)(2,1)} %all-to-all-done.arrived), custom_call_target="tpu_custom_call" | custom-call | tf_op jit(solution)/shard_map/collect/pallas_call | solution.py:563
  228.5 0.0 all-to-all-done.2
  228.5 0.8 convert_reduce_fusion
  (16 shorter events, 0.1 us)
Async XLA Ops:
  4.9 11.8 %copy-start.15 = (bf16[8,144,128]{2,1,0:T(8,128)(2,1)S(1)}, bf16[8,144,128]{2,1,0:T(8,128)(2,1)}, u32[]{:S(2)}) copy-start(bf16[8,144,128]{2,1,0:T(8,128)(2,1)} %get-tuple-element.24) | copy-start | bytes 884740
  5.0 12.7 %copy-start.14 = (bf16[8,144,128]{2,1,0:T(8,128)(2,1)S(1)}, bf16[8,144,128]{2,1,0:T(8,128)(2,1)}, u32[]{:S(2)}) copy-start(bf16[8,144,128]{2,1,0:T(8,128)(2,1)} %get-tuple-element.25) | copy-start | bytes 884740
  5.0 17.5 %copy-start.17 = (bf16[4,144,128]{2,1,0:T(8,128)(2,1)S(1)}, bf16[4,144,128]{2,1,0:T(8,128)(2,1)}, u32[]{:S(2)}) copy-start(bf16[4,144,128]{2,1,0:T(8,128)(2,1)} %get-tuple-element.26) | copy-start | bytes 442372
  5.0 17.4 %copy-start.16 = (bf16[4,144,128]{2,1,0:T(8,128)(2,1)S(1)}, bf16[4,144,128]{2,1,0:T(8,128)(2,1)}, u32[]{:S(2)}) copy-start(bf16[4,144,128]{2,1,0:T(8,128)(2,1)} %get-tuple-element.27) | copy-start | bytes 442372
  5.0 109.2 %all-to-all-start.1 = ((bf16[128,128,128]{2,1,0:T(8,128)(2,1)}), bf16[128,128,128]{2,1,0:T(8,128)(2,1)}, u32[]{:S(2)}, u32[]{:S(2)}) async-start(bf16[128,128,128]{2,1,0:T(8,128)(2,1)} %get-tuple-element.32), calls=%async_computation.1 | async-start | bytes 8388608 | tf_op jit(solution)/shard_map/all_to_all | solution.py:424
  16.7 55.7 %collective-permute-start = (bf16[8,144,128]{2,1,0:T(8,128)(2,1)S(1)}, bf16[8,144,128]{2,1,0:T(8,128)(2,1)S(1)}, u32[]{:S(2)}, u32[]{:S(2)}) collective-permute-start(bf16[8,144,128]{2,1,0:T(8,128)(2,1)S(1)} %copy-done.15), channel_id=1, source_target_pairs={{0,16},{1,17},{2,18},{3,19},{4,20},{5,21},{6,22},{7,23},{8,24},{9,... | collective-permute-start | bytes 884744 | tf_op jit(solution)/shard_map/ppermute | solution.py:420
  17.7 54.7 %collective-permute-start.1 = (bf16[8,144,128]{2,1,0:T(8,128)(2,1)S(1)}, bf16[8,144,128]{2,1,0:T(8,128)(2,1)S(1)}, u32[]{:S(2)}, u32[]{:S(2)}) collective-permute-start(bf16[8,144,128]{2,1,0:T(8,128)(2,1)S(1)} %copy-done.14), channel_id=1, source_target_pairs={{0,112},{1,113},{2,114},{3,115},{4,116},{5,117},{6,118},{7,119},{8... | collective-permute-start | bytes 884744 | tf_op jit(solution)/shard_map/ppermute | solution.py:420
  22.4 54.0 %collective-permute-start.2 = (bf16[4,144,128]{2,1,0:T(8,128)(2,1)S(1)}, bf16[4,144,128]{2,1,0:T(8,128)(2,1)S(1)}, u32[]{:S(2)}, u32[]{:S(2)}) collective-permute-start(bf16[4,144,128]{2,1,0:T(8,128)(2,1)S(1)} %copy-done.17), channel_id=1, source_target_pairs={{0,1},{1,2},{2,3},{3,4},{4,5},{5,6},{6,7},{7,8},{8,9},{9,10},{10,1... | collective-permute-start | bytes 442376 | tf_op jit(solution)/shard_map/ppermute | solution.py:420
  22.4 54.0 %collective-permute-start.3 = (bf16[4,144,128]{2,1,0:T(8,128)(2,1)S(1)}, bf16[4,144,128]{2,1,0:T(8,128)(2,1)S(1)}, u32[]{:S(2)}, u32[]{:S(2)}) collective-permute-start(bf16[4,144,128]{2,1,0:T(8,128)(2,1)S(1)} %copy-done.16), channel_id=1, source_target_pairs={{0,15},{1,0},{2,1},{3,2},{4,3},{5,4},{6,5},{7,6},{8,7},{9,8},{10,9... | collective-permute-start | bytes 442376 | tf_op jit(solution)/shard_map/ppermute | solution.py:420
  72.4 6.1 %copy-start = (bf16[8,144,128]{2,1,0:T(8,128)(2,1)}, bf16[8,144,128]{2,1,0:T(8,128)(2,1)S(1)}, u32[]{:S(2)}) copy-start(bf16[8,144,128]{2,1,0:T(8,128)(2,1)S(1)} %collective-permute-done.rest_0_) | copy-start | bytes 884740
  72.4 6.0 %copy-start.1 = (bf16[8,144,128]{2,1,0:T(8,128)(2,1)}, bf16[8,144,128]{2,1,0:T(8,128)(2,1)S(1)}, u32[]{:S(2)}) copy-start(bf16[8,144,128]{2,1,0:T(8,128)(2,1)S(1)} %collective-permute-done.1.rest_1_) | copy-start | bytes 884740
  72.5 6.0 %collective-permute-start.4 = (bf16[2,144,128]{2,1,0:T(8,128)(2,1)S(1)}, bf16[2,144,128]{2,1,0:T(8,128)(2,1)S(1)}, u32[]{:S(2)}, u32[]{:S(2)}) collective-permute-start(bf16[2,144,128]{2,1,0:T(8,128)(2,1)S(1)} %pad_maximum_fusion), channel_id=1, source_target_pairs={{0,1},{1,2},{2,3},{3,4},{4,5},{5,6},{6,7},{7,8},{8,9},{9,10},{10,1... | collective-permute-start | bytes 221192 | tf_op jit(solution)/shard_map/ppermute | solution.py:420
  72.6 5.9 %collective-permute-start.5 = (bf16[2,144,128]{2,1,0:T(8,128)(2,1)S(1)}, bf16[2,144,128]{2,1,0:T(8,128)(2,1)S(1)}, u32[]{:S(2)}, u32[]{:S(2)}) collective-permute-start(bf16[2,144,128]{2,1,0:T(8,128)(2,1)S(1)} %pad_maximum_fusion.1), channel_id=1, source_target_pairs={{0,15},{1,0},{2,1},{3,2},{4,3},{5,4},{6,5},{7,6},{8,7},{9,8},{10,9... | collective-permute-start | bytes 221192 | tf_op jit(solution)/shard_map/ppermute | solution.py:420
  76.5 2.0 copy-start.4
  76.5 2.0 copy-start.5
  78.4 0.6 copy-start.8
  78.5 0.6 copy-start.9
  114.2 60.0 %all-to-all-start = ((bf16[128,128,128]{2,1,0:T(8,128)(2,1)}), bf16[128,128,128]{2,1,0:T(8,128)(2,1)}, u32[]{:S(2)}, u32[]{:S(2)}) async-start(bf16[128,128,128]{2,1,0:T(8,128)(2,1)} %get-tuple-element.28), calls=%async_computation | async-start | bytes 8388608 | tf_op jit(solution)/shard_map/all_to_all | solution.py:424
  174.2 54.3 %all-to-all-start.2 = ((bf16[128,32,128]{2,1,0:T(8,128)(2,1)}), bf16[128,32,128]{2,1,0:T(8,128)(2,1)S(1)}, u32[]{:S(2)}, u32[]{:S(2)}) async-start(bf16[128,32,128]{2,1,0:T(8,128)(2,1)} %bitcast.10), calls=%async_computation.2 | async-start | bytes 2097152 | tf_op jit(solution)/shard_map/all_to_all | solution.py:424
  179.7 41.6 %collective-permute-start.6 = (bf16[8,128,128]{2,1,0:T(8,128)(2,1)}, bf16[8,128,128]{2,1,0:T(8,128)(2,1)S(1)}, u32[]{:S(2)}, u32[]{:S(2)}) collective-permute-start(bf16[8,128,128]{2,1,0:T(8,128)(2,1)} %get-tuple-element.34), channel_id=1, source_target_pairs={{0,16},{1,17},{2,18},{3,19},{4,20},{5,21},{6,22},{7,23},{8,24},{9,... | collective-permute-start | bytes 786440 | tf_op jit(solution)/shard_map/ppermute | solution.py:420
  180.7 40.6 %collective-permute-start.7 = (bf16[8,128,128]{2,1,0:T(8,128)(2,1)}, bf16[8,128,128]{2,1,0:T(8,128)(2,1)S(1)}, u32[]{:S(2)}, u32[]{:S(2)}) collective-permute-start(bf16[8,128,128]{2,1,0:T(8,128)(2,1)} %get-tuple-element.35), channel_id=1, source_target_pairs={{0,112},{1,113},{2,114},{3,115},{4,116},{5,117},{6,118},{7,119},{8... | collective-permute-start | bytes 786440 | tf_op jit(solution)/shard_map/ppermute | solution.py:420
  185.4 13.9 %collective-permute-start.10 = (bf16[1,128,128]{2,1,0:T(8,128)(2,1)}, bf16[1,128,128]{2,1,0:T(8,128)(2,1)S(1)}, u32[]{:S(2)}, u32[]{:S(2)}) collective-permute-start(bf16[1,128,128]{2,1,0:T(8,128)(2,1)} %get-tuple-element.38), channel_id=1, source_target_pairs={{0,17},{1,18},{2,19},{3,20},{4,21},{5,22},{6,23},{7,24},{8,25},{9,... | collective-permute-start | bytes 98312 | tf_op jit(solution)/shard_map/ppermute | solution.py:420
  185.4 35.9 %collective-permute-start.8 = (bf16[4,128,128]{2,1,0:T(8,128)(2,1)}, bf16[4,128,128]{2,1,0:T(8,128)(2,1)S(1)}, u32[]{:S(2)}, u32[]{:S(2)}) collective-permute-start(bf16[4,128,128]{2,1,0:T(8,128)(2,1)} %get-tuple-element.36), channel_id=1, source_target_pairs={{0,1},{1,2},{2,3},{3,4},{4,5},{5,6},{6,7},{7,8},{8,9},{9,10},{10,1... | collective-permute-start | bytes 393224 | tf_op jit(solution)/shard_map/ppermute | solution.py:420
  185.4 35.9 %collective-permute-start.9 = (bf16[4,128,128]{2,1,0:T(8,128)(2,1)}, bf16[4,128,128]{2,1,0:T(8,128)(2,1)S(1)}, u32[]{:S(2)}, u32[]{:S(2)}) collective-permute-start(bf16[4,128,128]{2,1,0:T(8,128)(2,1)} %get-tuple-element.37), channel_id=1, source_target_pairs={{0,15},{1,0},{2,1},{3,2},{4,3},{5,4},{6,5},{7,6},{8,7},{9,8},{10,9... | collective-permute-start | bytes 393224 | tf_op jit(solution)/shard_map/ppermute | solution.py:420
  199.3 22.1 %copy-start.10 = (bf16[1,128,128]{2,1,0:T(8,128)(2,1)}, bf16[1,128,128]{2,1,0:T(8,128)(2,1)S(1)}, u32[]{:S(2)}) copy-start(bf16[1,128,128]{2,1,0:T(8,128)(2,1)S(1)} %collective-permute-done.10.rest_4_) | copy-start | bytes 98308
  199.3 7.2 %collective-permute-start.11 = (bf16[1,128,128]{2,1,0:T(8,128)(2,1)}, bf16[1,128,128]{2,1,0:T(8,128)(2,1)S(1)}, u32[]{:S(2)}, u32[]{:S(2)}) collective-permute-start(bf16[1,128,128]{2,1,0:T(8,128)(2,1)} %get-tuple-element.39), channel_id=1, source_target_pairs={{0,31},{1,16},{2,17},{3,18},{4,19},{5,20},{6,21},{7,22},{8,23},{9,... | collective-permute-start | bytes 98312 | tf_op jit(solution)/shard_map/ppermute | solution.py:420
  206.5 14.9 %copy-start.11 = (bf16[1,128,128]{2,1,0:T(8,128)(2,1)}, bf16[1,128,128]{2,1,0:T(8,128)(2,1)S(1)}, u32[]{:S(2)}) copy-start(bf16[1,128,128]{2,1,0:T(8,128)(2,1)S(1)} %collective-permute-done.11.rest_5_) | copy-start | bytes 98308
  206.5 6.6 %collective-permute-start.12 = (bf16[1,128,128]{2,1,0:T(8,128)(2,1)}, bf16[1,128,128]{2,1,0:T(8,128)(2,1)S(1)}, u32[]{:S(2)}, u32[]{:S(2)}) collective-permute-start(bf16[1,128,128]{2,1,0:T(8,128)(2,1)} %get-tuple-element.40), channel_id=1, source_target_pairs={{0,113},{1,114},{2,115},{3,116},{4,117},{5,118},{6,119},{7,120},{8... | collective-permute-start | bytes 98312 | tf_op jit(solution)/shard_map/ppermute | solution.py:420
  213.1 8.4 %copy-start.12 = (bf16[1,128,128]{2,1,0:T(8,128)(2,1)}, bf16[1,128,128]{2,1,0:T(8,128)(2,1)S(1)}, u32[]{:S(2)}) copy-start(bf16[1,128,128]{2,1,0:T(8,128)(2,1)S(1)} %collective-permute-done.12.rest_6_) | copy-start | bytes 98308
  213.1 8.3 %collective-permute-start.13 = (bf16[1,128,128]{2,1,0:T(8,128)(2,1)}, bf16[1,128,128]{2,1,0:T(8,128)(2,1)S(1)}, u32[]{:S(2)}, u32[]{:S(2)}) collective-permute-start(bf16[1,128,128]{2,1,0:T(8,128)(2,1)} %get-tuple-element.41), channel_id=1, source_target_pairs={{0,127},{1,112},{2,113},{3,114},{4,115},{5,116},{6,117},{7,118},{8... | collective-permute-start | bytes 98312 | tf_op jit(solution)/shard_map/ppermute | solution.py:420
  221.3 0.6 copy-start.13
  221.3 0.7 copy-start.6
  221.3 0.7 copy-start.7
  221.4 0.8 copy-start.2
  221.4 0.8 copy-start.3

commit v3 on v2

--- a/solution.py
+++ b/solution.py
@@ -62,30 +62,50 @@
     return pltpu.CompilerParams(vmem_limit_bytes=VMEM_LIMIT, **extra)
 
 
-def pack_kernel(dims, counts, slots, features, positions, cotangent, *rest):
+def place_block(dims, counts, positions, r, c):
+    slot_count = dims[2]
+    lane = lax.broadcasted_iota(jnp.int32, (1, slot_count), 1)
+    place = [positions[r, axis, c : c + 1].astype(f32) for axis in range(3)]
+    place[0] = jnp.where(lane < counts[r, c], place[0], FAR)
+    pad = jnp.zeros((POS_ROWS - 3, slot_count), f32)
+    return jnp.concatenate(place + [pad], axis=0).astype(bf16)
+
+
+def side_kernel(dims, counts, features, positions, *rest):
+    rows, cols, slot_count = dims
+    sends, sem = rest[:SIDES], rest[SIDES]
+    copies = []
+    for step, send in zip(STEPS, sends):
+        for index, (r, c) in enumerate(border(step, rows, cols)):
+            copies.append(
+                pltpu.make_async_copy(
+                    features.at[r * cols + c],
+                    send.at[index, pl.ds(0, slot_count)],
+                    sem.at[len(copies)],
+                )
+            )
+    for copy in copies:
+        copy.start()
+    for step, send in zip(STEPS, sends):
+        for index, (r, c) in enumerate(border(step, rows, cols)):
+            send[index, slot_count:, :] = place_block(dims, counts, positions, r, c)
+    for copy in copies:
+        copy.wait()
+
+
+def pack_kernel(dims, counts, slots, features, positions, cotangent, home, packed, sem):
     rows, cols, slot_count = dims
     leaves = rows * cols
-    home, *sends = rest[: SIDES + 1]
-    packed, sem = rest[SIDES + 1 :]
     copies = [
         pltpu.make_async_copy(cotangent.at[g], packed.at[slots[g] // leaves], sem.at[g])
         for g in range(leaves)
     ]
     for copy in copies:
         copy.start()
-    lane = lax.broadcasted_iota(jnp.int32, (1, slot_count), 1)
-    pad = jnp.zeros((POS_ROWS - 3, slot_count), f32)
     for r in range(rows):
-        place = [positions[r, axis].astype(f32) for axis in range(3)]
         for c in range(cols):
-            leaf = r * cols + c
-            x = jnp.where(lane < counts[r, c], place[0][c : c + 1], FAR)
-            block = jnp.concatenate([x, place[1][c : c + 1], place[2][c : c + 1], pad], axis=0)
-            home[leaf, slot_count:, :] = block.astype(bf16)
+            home[r * cols + c, slot_count:, :] = place_block(dims, counts, positions, r, c)
     home[:, :slot_count, :] = features[...]
-    for step, send in zip(STEPS, sends):
-        for index, (r, c) in enumerate(border(step, rows, cols)):
-            send[index] = home[r * cols + c]
     for copy in copies:
         copy.wait()
 
@@ -387,16 +407,43 @@
             ).astype(grad.dtype)
 
 
+def corner_leaves(rows, cols):
+    return [(r, c) for r in (0, rows - 1) for c in (0, cols - 1)]
+
+
 def fold_kernel(dims, own, *rest):
     rows, cols = dims
-    received = rest[:8]
-    out, total = rest[8:]
+    received = rest[:SIDES]
+    out, corners, total = rest[SIDES:]
     total[...] = own[...]
     for step, piece in zip(STEPS, received):
         for index, (r, c) in enumerate(border((-step[0], -step[1]), rows, cols)):
             total[r * cols + c] += piece[index].astype(f32)
     for leaf in range(rows * cols):
         out[leaf] = total[leaf].T.astype(bf16)
+    for index, (r, c) in enumerate(corner_leaves(rows, cols)):
+        corners[index] = total[r * cols + c]
+
+
+def corner_kernel(dims, folded, corners, *rest):
+    rows, cols = dims
+    received = rest[: len(STEPS) - SIDES]
+    out, ready, sem = rest[len(STEPS) - SIDES :]
+    places = corner_leaves(rows, cols)
+    copies = []
+    for step, piece in zip(STEPS[SIDES:], received):
+        place = border((-step[0], -step[1]), rows, cols)[0]
+        index = places.index(place)
+        ready[index] = (corners[index] + piece[0].astype(f32)).T.astype(bf16)
+        copies.append(
+            pltpu.make_async_copy(
+                ready.at[index], out.at[place[0] * cols + place[1]], sem.at[index]
+            )
+        )
+    for copy in copies:
+        copy.start()
+    for copy in copies:
+        copy.wait()
 
 
 def collect_kernel(leaves, slots, arrived, out, sem):
@@ -452,24 +499,29 @@
     weight_rows = weights.reshape(width, channels)
     sizes = [len(border(step, rows, cols)) for step in STEPS]
 
-    home, *rest = pl.pallas_call(
+    flat = features.reshape(leaves, slot_count, channels)
+    places = positions.transpose(0, 2, 1, 3)
+    sends = pl.pallas_call(
+        functools.partial(side_kernel, (rows, cols, slot_count)),
+        out_shape=[jax.ShapeDtypeStruct((size, tall, channels), bf16) for size in sizes[:SIDES]],
+        in_specs=[smem(), hbm(), vmem()],
+        out_specs=[vmem()] * SIDES,
+        scratch_shapes=[any_dma((sum(sizes[:SIDES]),))],
+        compiler_params=params(),
+        name="pack_sides",
+    )(atom_counts, flat, places)
+    home, cot_packed = pl.pallas_call(
         functools.partial(pack_kernel, (rows, cols, slot_count)),
-        out_shape=[jax.ShapeDtypeStruct((leaves, tall, channels), bf16)]
-        + [jax.ShapeDtypeStruct((size, tall, channels), bf16) for size in sizes[:SIDES]]
-        + [jax.ShapeDtypeStruct((peers, slot_count, channels), bf16)],
+        out_shape=[
+            jax.ShapeDtypeStruct((leaves, tall, channels), bf16),
+            jax.ShapeDtypeStruct((peers, slot_count, channels), bf16),
+        ],
         in_specs=[smem(), smem(), vmem(), vmem(), vmem()],
-        out_specs=[vmem()] * (SIDES + 1) + [hbm()],
+        out_specs=[vmem(), hbm()],
         scratch_shapes=[any_dma((leaves,))],
         compiler_params=params(),
-        name="pack",
-    )(
-        atom_counts,
-        anchor,
-        features.reshape(leaves, slot_count, channels),
-        positions.transpose(0, 2, 1, 3),
-        cotangent,
-    )
-    sends, cot_packed = rest[:SIDES], rest[SIDES]
+        name="pack_rest",
+    )(atom_counts, anchor, flat, places, cotangent)
     halos = []
     for send, step in zip(sends, STEPS):
         halos.append(shift(send, step, shape))
@@ -550,15 +602,31 @@
     received = []
     for send, step in zip(grad_sends, STEPS):
         received.append(shift(send, step, shape))
+    folded, corners = pl.pallas_call(
+        functools.partial(fold_kernel, (rows, cols)),
+        out_shape=[
+            jax.ShapeDtypeStruct((leaves, slot_count, channels), bf16),
+            jax.ShapeDtypeStruct((len(STEPS) - SIDES, channels, slot_count), f32),
+        ],
+        in_specs=[vmem()] * (SIDES + 1),
+        out_specs=[vmem(), vmem()],
+        scratch_shapes=[pltpu.VMEM((leaves, channels, slot_count), f32)],
+        compiler_params=params(),
+        name="fold_sides",
+    )(own, *received[:SIDES])
     feature_grad = pl.pallas_call(
-        functools.partial(fold_kernel, (rows, cols)),
+        functools.partial(corner_kernel, (rows, cols)),
         out_shape=jax.ShapeDtypeStruct((leaves, slot_count, channels), bf16),
-        in_specs=[vmem()] * 9,
-        out_specs=vmem(),
-        scratch_shapes=[pltpu.VMEM((leaves, slot_count, channels), f32)],
+        in_specs=[hbm()] + [vmem()] * (len(STEPS) - SIDES + 1),
+        out_specs=hbm(),
+        scratch_shapes=[
+            pltpu.VMEM((len(STEPS) - SIDES, slot_count, channels), bf16),
+            any_dma((len(STEPS) - SIDES,)),
+        ],
+        input_output_aliases={0: 0},
         compiler_params=params(),
-        name="fold",
-    )(own, *received)
+        name="fold_corners",
+    )(folded, corners, *received[SIDES:])
 
     updated = pl.pallas_call(
         functools.partial(collect_kernel, leaves),

time: 232 us -> 221 us (0.953)
  waiting for transfers between devices: 83.5 us -> 71.4 us
  Pallas kernels: 84.3 us -> 88.6 us
    ppermute x14, waiting for transfers between devices: 70 us -> 57.9 us  [shift(): return lax.ppermute(value, AXES, pairs)]
    pallas_call x1 -> x3, Pallas kernels: 3.13 us -> 7.82 us  [the longest x1 3.1 us: shards(): pl.pallas_call(functools.partial(fold_kernel, (rows, cols)), out_shape=[j...]
  transfers between devices with their start and end apart: 17 -> 17, of which waited for: 7 -> 4; matrix products, arithmetic and copies ran while one was open for 0% -> 0% of each run, Pallas kernels for 35% -> 38%
where the time goes in v3:
time: 221 us; the launch traced here: 220 us
  Pallas kernels  88.6 us (40%)
  waiting for transfers between devices  71.4 us (32%)
  starting transfers between devices  56.6 us (26%)
    ppermute x14, waiting for transfers between devices, shift(): return lax.ppermute(value, AXES, pairs)  57.9 us
    pallas_call x1, Pallas kernels, shards(): pl.pallas_call(functools.partial(backward_kernel, (rows, cols, slot_count...  38.7 us
    pallas_call x1, Pallas kernels, shards(): pl.pallas_call(functools.partial(forward_kernel, (rows, cols, slot_count,...  35 us
    ppermute x14, starting transfers between devices, shift(): return lax.ppermute(value, AXES, pairs)  31.5 us
    all_to_all x3, starting transfers between devices, relay(): return lax.all_to_all(buffer, AXES, split_axis=0, concat_axis=0, tiled=True)  25.1 us
    all_to_all x3, waiting for transfers between devices, relay(): return lax.all_to_all(buffer, AXES, split_axis=0, concat_axis=0, tiled=True)  13.5 us
  transfers between devices with their start and end apart: 17, of which 4 were waited for; matrix products, arithmetic and copies ran while one was open for 0% of the time, Pallas kernels for 38%

profile of v3, /device:TPU:0, one launch (start us, length us, event | category | flops | bytes accessed | tf_op | source)
XLA Modules:
  0.0 220.2 jit_solution(2149542844944614671)
XLA Ops:
  0.6 3.9 %pack_rest.1 = (bf16[32,144,128]{2,1,0:T(8,128)(2,1)}, bf16[128,128,128]{2,1,0:T(8,128)(2,1)}) custom-call(s32[4,8]{1,0:T(4,128)} %counts.5, s32[32]{0:T(128)} %slots.6, bf16[32,128,128]{2,1,0:T(8,128)(2,1)} %bitcast.9, bf16[4,3,8,128]{3,2,1,0:T(8,128)(2,1)} %bitcast.15, bf16[32,128,128]{2,1,0:T(8,128)(2,1)} %cotangent.1), custom_call_target="tpu_custom_call" | custom-call | tf_op jit(solution)/shard_map/pack_rest/pallas_call | solution.py:513
  4.5 11.7 %all-to-all-start.1 = ((bf16[128,128,128]{2,1,0:T(8,128)(2,1)}), bf16[128,128,128]{2,1,0:T(8,128)(2,1)}, u32[]{:S(2)}, u32[]{:S(2)}) async-start(bf16[128,128,128]{2,1,0:T(8,128)(2,1)} %get-tuple-element.34), calls=%async_computation.1 | async-start | bytes 8388608 | tf_op jit(solution)/shard_map/all_to_all | solution.py:471
  16.3 2.9 %pack_sides.1 = (bf16[8,144,128]{2,1,0:T(8,128)(2,1)}, bf16[8,144,128]{2,1,0:T(8,128)(2,1)}, bf16[4,144,128]{2,1,0:T(8,128)(2,1)}, bf16[4,144,128]{2,1,0:T(8,128)(2,1)}) custom-call(s32[4,8]{1,0:T(4,128)} %counts.5, bf16[32,128,128]{2,1,0:T(8,128)(2,1)} %bitcast.10, bf16[4,3,8,128]{3,2,1,0:T(8,128)(2,1)} %bitcast.16), custom_call_target="tpu_custom_call" | custom-call | tf_op jit(solution)/shard_map/pack_sides/pallas_call | solution.py:504
  19.3 1.0 collective-permute-start
  20.2 4.8 %collective-permute-start.1 = (bf16[8,144,128]{2,1,0:T(8,128)(2,1)}, bf16[8,144,128]{2,1,0:T(8,128)(2,1)S(1)}, u32[]{:S(2)}, u32[]{:S(2)}) collective-permute-start(bf16[8,144,128]{2,1,0:T(8,128)(2,1)} %get-tuple-element.27), channel_id=1, source_target_pairs={{0,112},{1,113},{2,114},{3,115},{4,116},{5,117},{6,118},{7,119},{8... | collective-permute-start | bytes 884744 | tf_op jit(solution)/shard_map/ppermute | solution.py:467
  25.0 0.0 collective-permute-start.2
  25.0 3.9 %collective-permute-start.3 = (bf16[4,144,128]{2,1,0:T(8,128)(2,1)}, bf16[4,144,128]{2,1,0:T(8,128)(2,1)S(1)}, u32[]{:S(2)}, u32[]{:S(2)}) collective-permute-start(bf16[4,144,128]{2,1,0:T(8,128)(2,1)} %get-tuple-element.29), channel_id=1, source_target_pairs={{0,15},{1,0},{2,1},{3,2},{4,3},{5,4},{6,5},{7,6},{8,7},{9,8},{10,9... | collective-permute-start | bytes 442376 | tf_op jit(solution)/shard_map/ppermute | solution.py:467
  28.8 43.2 %collective-permute-done.rest_0_ = bf16[8,144,128]{2,1,0:T(8,128)(2,1)S(1)} collective-permute-done((bf16[8,144,128]{2,1,0:T(8,128)(2,1)}, bf16[8,144,128]{2,1,0:T(8,128)(2,1)S(1)}, u32[]{:S(2)}, u32[]{:S(2)}) %collective-permute-start) | collective-permute-done | bytes 294944 | tf_op jit(solution)/shard_map/ppermute | solution.py:467
  72.0 0.0 copy-start
  72.0 0.0 collective-permute-done.1.rest_1_
  72.0 0.0 copy-start.1
  72.1 0.1 collective-permute-start.4
  72.2 3.9 %collective-permute-start.5 = (bf16[2,144,128]{2,1,0:T(8,128)(2,1)S(1)}, bf16[2,144,128]{2,1,0:T(8,128)(2,1)S(1)}, u32[]{:S(2)}, u32[]{:S(2)}) collective-permute-start(bf16[2,144,128]{2,1,0:T(8,128)(2,1)S(1)} %pad_maximum_fusion.1), channel_id=1, source_target_pairs={{0,15},{1,0},{2,1},{3,2},{4,3},{5,4},{6,5},{7,6},{8,7},{9,8},{10,9... | collective-permute-start | bytes 221192 | tf_op jit(solution)/shard_map/ppermute | solution.py:467
  76.1 0.0 collective-permute-done.2.rest_2_
  76.1 0.0 copy-start.4
  76.1 0.0 collective-permute-done.3.rest_3_
  76.1 0.0 copy-start.5
  76.1 1.9 collective-permute-done.4.rest_4_
  78.0 0.0 collective-permute-done.5.rest_5_
  78.1 0.0 copy-done
  78.1 0.0 copy-done.1
  78.1 0.0 copy-done.4
  78.1 0.0 copy-done.5
  78.1 0.6 copy-done.8
  78.7 0.0 copy-done.9
  78.7 35.0 %forward.1 = (f32[128,4096]{1,0:T(8,128)}, bf16[128,128,128]{2,1,0:T(8,128)(2,1)}, bf16[32,4096,128]{2,1,0:T(8,128)(2,1)}, bf16[128,128,128]{2,1,0:T(8,128)(2,1)}) custom-call(s32[4,4,8]{2,1,0:T(4,128)} %bitcast.17, s32[4,8]{1,0:T(4,128)} %counts.5, s32[4,8]{1,0:T(4,128)} %slots.7, bf16[32,144,128]{2,1,0:T(8,128)(2,1)} %get-tuple-element.25.home, ...), custom_call_target="tpu_custom_call" | custom-call | tf_op jit(solution)/shard_map/forward/pallas_call | solution.py:534
  113.7 0.0 all-to-all-done.1.returned
  113.7 7.9 %all-to-all-start = ((bf16[128,128,128]{2,1,0:T(8,128)(2,1)}), bf16[128,128,128]{2,1,0:T(8,128)(2,1)}, u32[]{:S(2)}, u32[]{:S(2)}) async-start(bf16[128,128,128]{2,1,0:T(8,128)(2,1)} %get-tuple-element.30), calls=%async_computation | async-start | bytes 8388608 | tf_op jit(solution)/shard_map/all_to_all | solution.py:471
  121.6 38.7 %backward.1 = (f32[32,128,128]{2,1,0:T(8,128)}, bf16[4096,128]{1,0:T(8,128)(2,1)}, bf16[8,128,128]{2,1,0:T(8,128)(2,1)}, bf16[8,128,128]{2,1,0:T(8,128)(2,1)}, b...) custom-call(s32[4,4,8]{2,1,0:T(4,128)} %bitcast.18, ...), custom_call_target="tpu_custom_call" | custom-call | tf_op jit(solution)/shard_map/backward/pallas_call | solution.py:565
  160.3 13.5 %all-to-all-done.arrived = bf16[128,128,128]{2,1,0:T(8,128)(2,1)} async-done(((bf16[128,128,128]{2,1,0:T(8,128)(2,1)}), bf16[128,128,128]{2,1,0:T(8,128)(2,1)}, u32[]{:S(2)}, u32[]{:S(2)}) %all-to-all-start) | async-done | bytes 4194336 | tf_op jit(solution)/shard_map/all_to_all | solution.py:471
  173.8 5.5 %all-to-all-start.2 = ((bf16[128,32,128]{2,1,0:T(8,128)(2,1)}), bf16[128,32,128]{2,1,0:T(8,128)(2,1)S(1)}, u32[]{:S(2)}, u32[]{:S(2)}) async-start(bf16[128,32,128]{2,1,0:T(8,128)(2,1)} %bitcast.11), calls=%async_computation.2 | async-start | bytes 2097152 | tf_op jit(solution)/shard_map/all_to_all | solution.py:471
  179.3 1.0 collective-permute-start.6
  180.3 4.7 %collective-permute-start.7 = (bf16[8,128,128]{2,1,0:T(8,128)(2,1)}, bf16[8,128,128]{2,1,0:T(8,128)(2,1)S(1)}, u32[]{:S(2)}, u32[]{:S(2)}) collective-permute-start(bf16[8,128,128]{2,1,0:T(8,128)(2,1)} %get-tuple-element.37), channel_id=1, source_target_pairs={{0,112},{1,113},{2,114},{3,115},{4,116},{5,117},{6,118},{7,119},{8... | collective-permute-start | bytes 786440 | tf_op jit(solution)/shard_map/ppermute | solution.py:467
  185.0 0.0 collective-permute-start.8
  185.0 3.9 %collective-permute-start.9 = (bf16[4,128,128]{2,1,0:T(8,128)(2,1)}, bf16[4,128,128]{2,1,0:T(8,128)(2,1)S(1)}, u32[]{:S(2)}, u32[]{:S(2)}) collective-permute-start(bf16[4,128,128]{2,1,0:T(8,128)(2,1)} %get-tuple-element.39), channel_id=1, source_target_pairs={{0,15},{1,0},{2,1},{3,2},{4,3},{5,4},{6,5},{7,6},{8,7},{9,8},{10,9... | collective-permute-start | bytes 393224 | tf_op jit(solution)/shard_map/ppermute | solution.py:467
  188.8 0.0 collective-permute-start.10
  188.8 12.7 %collective-permute-done.8.rest_2_ = bf16[4,128,128]{2,1,0:T(8,128)(2,1)S(1)} collective-permute-done((bf16[4,128,128]{2,1,0:T(8,128)(2,1)}, bf16[4,128,128]{2,1,0:T(8,128)(2,1)S(1)}, u32[]{:S(2)}, u32[]{:S(2)}) %collective-permute-start.8) | collective-permute-done | bytes 131104 | tf_op jit(solution)/shard_map/ppermute | solution.py:467
  201.6 0.0 collective-permute-start.11
  201.6 0.0 collective-permute-done.9.rest_3_
  201.6 0.0 copy-start.7
  201.6 5.3 %collective-permute-start.12 = (bf16[1,128,128]{2,1,0:T(8,128)(2,1)}, bf16[1,128,128]{2,1,0:T(8,128)(2,1)S(1)}, u32[]{:S(2)}, u32[]{:S(2)}) collective-permute-start(bf16[1,128,128]{2,1,0:T(8,128)(2,1)} %get-tuple-element.44), channel_id=1, source_target_pairs={{0,113},{1,114},{2,115},{3,116},{4,117},{5,118},{6,119},{7,120},{8... | collective-permute-start | bytes 98312 | tf_op jit(solution)/shard_map/ppermute | solution.py:467
  207.0 0.0 collective-permute-done.6.rest_0_
  207.0 3.0 %collective-permute-start.13 = (bf16[1,128,128]{2,1,0:T(8,128)(2,1)}, bf16[1,128,128]{2,1,0:T(8,128)(2,1)S(1)}, u32[]{:S(2)}, u32[]{:S(2)}) collective-permute-start(bf16[1,128,128]{2,1,0:T(8,128)(2,1)} %get-tuple-element.45), channel_id=1, source_target_pairs={{0,127},{1,112},{2,113},{3,114},{4,115},{5,116},{6,117},{7,118},{8... | collective-permute-start | bytes 98312 | tf_op jit(solution)/shard_map/ppermute | solution.py:467
  210.0 0.0 collective-permute-done.7.rest_1_
  210.0 0.0 copy-done.6
  210.0 0.0 copy-done.7
  210.0 0.0 copy-done.2
  210.0 0.7 copy-done.3
  210.7 3.1 %fold_sides.1 = (bf16[32,128,128]{2,1,0:T(8,128)(2,1)}, f32[4,128,128]{2,1,0:T(8,128)}) custom-call(f32[32,128,128]{2,1,0:T(8,128)} %get-tuple-element.35.own, bf16[8,128,128]{2,1,0:T(8,128)(2,1)} %copy-done.2, bf16[8,128,128]{2,1,0:T(8,128)(2,1)} %copy-done.3, bf16[4,128,128]{2,1,0:T(8,128)(2,1)} %copy-done.6, bf16[4,128,128]{2,1,0:T(8,128)(2,1)} %copy-done.7), custom_call_target="tpu_custom_call" | custom-call | tf_op jit(solution)/shard_map/fold_sides/pallas_call | solution.py:605
  213.8 0.0 collective-permute-done.10.rest_0_
  213.8 0.0 collective-permute-done.11.rest_1_
  213.8 0.0 copy-start.11
  213.8 0.0 collective-permute-done.12.rest_2_
  213.8 0.0 copy-start.12
  213.8 0.0 collective-permute-done.13.rest_3_
  213.8 0.0 copy-start.13
  213.9 0.5 copy-done.10
  214.4 0.0 copy-done.11
  214.4 0.0 copy-done.12
  214.4 0.0 copy-done.13
  214.5 1.8 fold_corners.1
  216.3 3.1 %collect.1 = bf16[32,128,128]{2,1,0:T(8,128)(2,1)} custom-call(s32[32]{0:T(128)} %slots.6, bf16[128,128,128]{2,1,0:T(8,128)(2,1)} %all-to-all-done.arrived), custom_call_target="tpu_custom_call" | custom-call | tf_op jit(solution)/shard_map/collect/pallas_call | solution.py:631
  219.4 0.0 all-to-all-done.2
  219.4 0.8 convert_reduce_fusion
  (10 shorter events, 0.0 us)
Async XLA Ops:
  4.5 109.2 %all-to-all-start.1 = ((bf16[128,128,128]{2,1,0:T(8,128)(2,1)}), bf16[128,128,128]{2,1,0:T(8,128)(2,1)}, u32[]{:S(2)}, u32[]{:S(2)}) async-start(bf16[128,128,128]{2,1,0:T(8,128)(2,1)} %get-tuple-element.34), calls=%async_computation.1 | async-start | bytes 8388608 | tf_op jit(solution)/shard_map/all_to_all | solution.py:471
  19.3 52.7 %collective-permute-start = (bf16[8,144,128]{2,1,0:T(8,128)(2,1)}, bf16[8,144,128]{2,1,0:T(8,128)(2,1)S(1)}, u32[]{:S(2)}, u32[]{:S(2)}) collective-permute-start(bf16[8,144,128]{2,1,0:T(8,128)(2,1)} %get-tuple-element.26), channel_id=1, source_target_pairs={{0,16},{1,17},{2,18},{3,19},{4,20},{5,21},{6,22},{7,23},{8,24},{9,... | collective-permute-start | bytes 884744 | tf_op jit(solution)/shard_map/ppermute | solution.py:467
  20.2 51.8 %collective-permute-start.1 = (bf16[8,144,128]{2,1,0:T(8,128)(2,1)}, bf16[8,144,128]{2,1,0:T(8,128)(2,1)S(1)}, u32[]{:S(2)}, u32[]{:S(2)}) collective-permute-start(bf16[8,144,128]{2,1,0:T(8,128)(2,1)} %get-tuple-element.27), channel_id=1, source_target_pairs={{0,112},{1,113},{2,114},{3,115},{4,116},{5,117},{6,118},{7,119},{8... | collective-permute-start | bytes 884744 | tf_op jit(solution)/shard_map/ppermute | solution.py:467
  25.0 51.1 %collective-permute-start.2 = (bf16[4,144,128]{2,1,0:T(8,128)(2,1)}, bf16[4,144,128]{2,1,0:T(8,128)(2,1)S(1)}, u32[]{:S(2)}, u32[]{:S(2)}) collective-permute-start(bf16[4,144,128]{2,1,0:T(8,128)(2,1)} %get-tuple-element.28), channel_id=1, source_target_pairs={{0,1},{1,2},{2,3},{3,4},{4,5},{5,6},{6,7},{7,8},{8,9},{9,10},{10,1... | collective-permute-start | bytes 442376 | tf_op jit(solution)/shard_map/ppermute | solution.py:467
  25.0 51.1 %collective-permute-start.3 = (bf16[4,144,128]{2,1,0:T(8,128)(2,1)}, bf16[4,144,128]{2,1,0:T(8,128)(2,1)S(1)}, u32[]{:S(2)}, u32[]{:S(2)}) collective-permute-start(bf16[4,144,128]{2,1,0:T(8,128)(2,1)} %get-tuple-element.29), channel_id=1, source_target_pairs={{0,15},{1,0},{2,1},{3,2},{4,3},{5,4},{6,5},{7,6},{8,7},{9,8},{10,9... | collective-permute-start | bytes 442376 | tf_op jit(solution)/shard_map/ppermute | solution.py:467
  72.0 6.1 %copy-start = (bf16[8,144,128]{2,1,0:T(8,128)(2,1)}, bf16[8,144,128]{2,1,0:T(8,128)(2,1)S(1)}, u32[]{:S(2)}) copy-start(bf16[8,144,128]{2,1,0:T(8,128)(2,1)S(1)} %collective-permute-done.rest_0_) | copy-start | bytes 884740
  72.0 6.0 %copy-start.1 = (bf16[8,144,128]{2,1,0:T(8,128)(2,1)}, bf16[8,144,128]{2,1,0:T(8,128)(2,1)S(1)}, u32[]{:S(2)}) copy-start(bf16[8,144,128]{2,1,0:T(8,128)(2,1)S(1)} %collective-permute-done.1.rest_1_) | copy-start | bytes 884740
  72.1 6.0 %collective-permute-start.4 = (bf16[2,144,128]{2,1,0:T(8,128)(2,1)S(1)}, bf16[2,144,128]{2,1,0:T(8,128)(2,1)S(1)}, u32[]{:S(2)}, u32[]{:S(2)}) collective-permute-start(bf16[2,144,128]{2,1,0:T(8,128)(2,1)S(1)} %pad_maximum_fusion), channel_id=1, source_target_pairs={{0,1},{1,2},{2,3},{3,4},{4,5},{5,6},{6,7},{7,8},{8,9},{9,10},{10,1... | collective-permute-start | bytes 221192 | tf_op jit(solution)/shard_map/ppermute | solution.py:467
  72.2 5.9 %collective-permute-start.5 = (bf16[2,144,128]{2,1,0:T(8,128)(2,1)S(1)}, bf16[2,144,128]{2,1,0:T(8,128)(2,1)S(1)}, u32[]{:S(2)}, u32[]{:S(2)}) collective-permute-start(bf16[2,144,128]{2,1,0:T(8,128)(2,1)S(1)} %pad_maximum_fusion.1), channel_id=1, source_target_pairs={{0,15},{1,0},{2,1},{3,2},{4,3},{5,4},{6,5},{7,6},{8,7},{9,8},{10,9... | collective-permute-start | bytes 221192 | tf_op jit(solution)/shard_map/ppermute | solution.py:467
  76.1 2.0 copy-start.4
  76.1 2.0 copy-start.5
  78.0 0.6 copy-start.8
  78.1 0.6 copy-start.9
  113.7 60.0 %all-to-all-start = ((bf16[128,128,128]{2,1,0:T(8,128)(2,1)}), bf16[128,128,128]{2,1,0:T(8,128)(2,1)}, u32[]{:S(2)}, u32[]{:S(2)}) async-start(bf16[128,128,128]{2,1,0:T(8,128)(2,1)} %get-tuple-element.30), calls=%async_computation | async-start | bytes 8388608 | tf_op jit(solution)/shard_map/all_to_all | solution.py:471
  173.8 45.6 %all-to-all-start.2 = ((bf16[128,32,128]{2,1,0:T(8,128)(2,1)}), bf16[128,32,128]{2,1,0:T(8,128)(2,1)S(1)}, u32[]{:S(2)}, u32[]{:S(2)}) async-start(bf16[128,32,128]{2,1,0:T(8,128)(2,1)} %bitcast.11), calls=%async_computation.2 | async-start | bytes 2097152 | tf_op jit(solution)/shard_map/all_to_all | solution.py:471
  179.3 27.7 %collective-permute-start.6 = (bf16[8,128,128]{2,1,0:T(8,128)(2,1)}, bf16[8,128,128]{2,1,0:T(8,128)(2,1)S(1)}, u32[]{:S(2)}, u32[]{:S(2)}) collective-permute-start(bf16[8,128,128]{2,1,0:T(8,128)(2,1)} %get-tuple-element.36), channel_id=1, source_target_pairs={{0,16},{1,17},{2,18},{3,19},{4,20},{5,21},{6,22},{7,23},{8,24},{9,... | collective-permute-start | bytes 786440 | tf_op jit(solution)/shard_map/ppermute | solution.py:467
  180.3 29.7 %collective-permute-start.7 = (bf16[8,128,128]{2,1,0:T(8,128)(2,1)}, bf16[8,128,128]{2,1,0:T(8,128)(2,1)S(1)}, u32[]{:S(2)}, u32[]{:S(2)}) collective-permute-start(bf16[8,128,128]{2,1,0:T(8,128)(2,1)} %get-tuple-element.37), channel_id=1, source_target_pairs={{0,112},{1,113},{2,114},{3,115},{4,116},{5,117},{6,118},{7,119},{8... | collective-permute-start | bytes 786440 | tf_op jit(solution)/shard_map/ppermute | solution.py:467
  185.0 16.6 %collective-permute-start.8 = (bf16[4,128,128]{2,1,0:T(8,128)(2,1)}, bf16[4,128,128]{2,1,0:T(8,128)(2,1)S(1)}, u32[]{:S(2)}, u32[]{:S(2)}) collective-permute-start(bf16[4,128,128]{2,1,0:T(8,128)(2,1)} %get-tuple-element.38), channel_id=1, source_target_pairs={{0,1},{1,2},{2,3},{3,4},{4,5},{5,6},{6,7},{7,8},{8,9},{9,10},{10,1... | collective-permute-start | bytes 393224 | tf_op jit(solution)/shard_map/ppermute | solution.py:467
  185.0 16.6 %collective-permute-start.9 = (bf16[4,128,128]{2,1,0:T(8,128)(2,1)}, bf16[4,128,128]{2,1,0:T(8,128)(2,1)S(1)}, u32[]{:S(2)}, u32[]{:S(2)}) collective-permute-start(bf16[4,128,128]{2,1,0:T(8,128)(2,1)} %get-tuple-element.39), channel_id=1, source_target_pairs={{0,15},{1,0},{2,1},{3,2},{4,3},{5,4},{6,5},{7,6},{8,7},{9,8},{10,9... | collective-permute-start | bytes 393224 | tf_op jit(solution)/shard_map/ppermute | solution.py:467
  188.8 25.0 %collective-permute-start.10 = (bf16[1,128,128]{2,1,0:T(8,128)(2,1)}, bf16[1,128,128]{2,1,0:T(8,128)(2,1)S(1)}, u32[]{:S(2)}, u32[]{:S(2)}) collective-permute-start(bf16[1,128,128]{2,1,0:T(8,128)(2,1)} %get-tuple-element.42), channel_id=1, source_target_pairs={{0,17},{1,18},{2,19},{3,20},{4,21},{5,22},{6,23},{7,24},{8,25},{9,... | collective-permute-start | bytes 98312 | tf_op jit(solution)/shard_map/ppermute | solution.py:467
  201.6 8.4 %copy-start.6 = (bf16[4,128,128]{2,1,0:T(8,128)(2,1)}, bf16[4,128,128]{2,1,0:T(8,128)(2,1)S(1)}, u32[]{:S(2)}) copy-start(bf16[4,128,128]{2,1,0:T(8,128)(2,1)S(1)} %collective-permute-done.8.rest_2_) | copy-start | bytes 393220
  201.6 12.2 %collective-permute-start.11 = (bf16[1,128,128]{2,1,0:T(8,128)(2,1)}, bf16[1,128,128]{2,1,0:T(8,128)(2,1)S(1)}, u32[]{:S(2)}, u32[]{:S(2)}) collective-permute-start(bf16[1,128,128]{2,1,0:T(8,128)(2,1)} %get-tuple-element.43), channel_id=1, source_target_pairs={{0,31},{1,16},{2,17},{3,18},{4,19},{5,20},{6,21},{7,22},{8,23},{9,... | collective-permute-start | bytes 98312 | tf_op jit(solution)/shard_map/ppermute | solution.py:467
  201.6 8.4 %copy-start.7 = (bf16[4,128,128]{2,1,0:T(8,128)(2,1)}, bf16[4,128,128]{2,1,0:T(8,128)(2,1)S(1)}, u32[]{:S(2)}) copy-start(bf16[4,128,128]{2,1,0:T(8,128)(2,1)S(1)} %collective-permute-done.9.rest_3_) | copy-start | bytes 393220
  201.6 12.2 %collective-permute-start.12 = (bf16[1,128,128]{2,1,0:T(8,128)(2,1)}, bf16[1,128,128]{2,1,0:T(8,128)(2,1)S(1)}, u32[]{:S(2)}, u32[]{:S(2)}) collective-permute-start(bf16[1,128,128]{2,1,0:T(8,128)(2,1)} %get-tuple-element.44), channel_id=1, source_target_pairs={{0,113},{1,114},{2,115},{3,116},{4,117},{5,118},{6,119},{7,120},{8... | collective-permute-start | bytes 98312 | tf_op jit(solution)/shard_map/ppermute | solution.py:467
  207.0 3.0 %copy-start.2 = (bf16[8,128,128]{2,1,0:T(8,128)(2,1)}, bf16[8,128,128]{2,1,0:T(8,128)(2,1)S(1)}, u32[]{:S(2)}) copy-start(bf16[8,128,128]{2,1,0:T(8,128)(2,1)S(1)} %collective-permute-done.6.rest_0_) | copy-start | bytes 786436
  207.0 6.9 %collective-permute-start.13 = (bf16[1,128,128]{2,1,0:T(8,128)(2,1)}, bf16[1,128,128]{2,1,0:T(8,128)(2,1)S(1)}, u32[]{:S(2)}, u32[]{:S(2)}) collective-permute-start(bf16[1,128,128]{2,1,0:T(8,128)(2,1)} %get-tuple-element.45), channel_id=1, source_target_pairs={{0,127},{1,112},{2,113},{3,114},{4,115},{5,116},{6,117},{7,118},{8... | collective-permute-start | bytes 98312 | tf_op jit(solution)/shard_map/ppermute | solution.py:467
  210.0 0.7 copy-start.3
  213.8 0.6 copy-start.10
  213.8 0.6 copy-start.11
  213.8 0.6 copy-start.12
  213.8 0.6 copy-start.13
